TPU v7x, 32 devices: a whole 2x2x4 slice. The times are simulated.
32 devices in a mesh: rep: 4 (over y, core), shard: 8 (over z, x).
Axes of the slice: x: 2, y: 2, z: 4, core: 2. Of those that a mesh axis runs over, the one named last changes fastest.
Arguments:
- layer_input: bfloat16 [32, 197, 768], P(('rep', 'shard')), may hold values from -6 to 6
- cotangent: bfloat16 [32, 197, 768], P(('rep', 'shard')), may hold values from -6 to 6
- live: int32 [32], P(('rep', 'shard')), may hold values 0 or 1
- first_gain: bfloat16 [768], P('shard'), may hold values from 0.099609375 to 1.8984375
- first_bias: bfloat16 [768], P('shard'), may hold values from -3 to 3
- qkv_weight: bfloat16 [768, 2304], P('shard'), may hold values from -0.21875 to 0.21875
- query_bias: bfloat16 [768], P('shard'), may hold values from -3 to 3
- value_bias: bfloat16 [768], P('shard'), may hold values from -3 to 3
- out_weight: bfloat16 [768, 768], P('shard'), may hold values from -1.5 to 1.5
- out_bias: bfloat16 [768], P('shard'), may hold values from -3 to 3
- second_gain: bfloat16 [768], P('shard'), may hold values from 0.099609375 to 1.8984375
- second_bias: bfloat16 [768], P('shard'), may hold values from -3 to 3
- up_weight: bfloat16 [768, 3072], P('shard'), may hold values from -0.21875 to 0.21875
- up_bias: bfloat16 [3072], P('shard'), may hold values from -3 to 3
- down_weight: bfloat16 [3072, 768], P('shard'), may hold values from -0.109375 to 0.109375
- down_bias: bfloat16 [768], P('shard'), may hold values from -3 to 3
Outputs:
- output: bfloat16 [32, 197, 768], P(('rep', 'shard'))
- input_grad: bfloat16 [32, 197, 768], P(('rep', 'shard'))
- first_gain_grad: float32 [768], P('shard')
- first_bias_grad: float32 [768], P('shard')
- qkv_weight_grad: float32 [768, 2304], P('shard')
- query_bias_grad: float32 [768], P('shard')
- value_bias_grad: float32 [768], P('shard')
- out_weight_grad: float32 [768, 768], P('shard')
- out_bias_grad: float32 [768], P('shard')
- second_gain_grad: float32 [768], P('shard')
- second_bias_grad: float32 [768], P('shard')
- up_weight_grad: float32 [768, 3072], P('shard')
- up_bias_grad: float32 [3072], P('shard')
- down_weight_grad: float32 [3072, 768], P('shard')
- down_bias_grad: float32 [768], P('shard')
All inputs are finite; a program needn't handle non-finite values. No bound on the sum of `live` on one device may be relied on, other than what follows from the above.
Results may differ from a plain program's by a relative error of at most 0.014.
Values may be sent and summed in bfloat16 or wider, within the bound.
A program may use at most 128 MiB of HBM per device.

v0:
```python
import jax
import jax.numpy as jnp
from jax import lax
from jax.sharding import PartitionSpec as P

HEAD_DIM = 64


norm_eps = 1e-06
root_half = 0.7071067811865476
density_coef = 0.3989422804014327


def matmul(operand, factor):
    flat = operand.reshape(-1, operand.shape[-1])
    product = jnp.dot(flat, factor, preferred_element_type=jnp.float32)
    return product.reshape(operand.shape[:-1] + (factor.shape[-1],))


def outer_product(operand, factor):
    return jnp.dot(
        operand.reshape(-1, operand.shape[-1]).T,
        factor.reshape(-1, factor.shape[-1]),
        preferred_element_type=jnp.float32,
    )


def batched(form, operand, factor):
    return jnp.einsum(form, operand, factor, preferred_element_type=jnp.float32)


def layer_norm(values, norm_gain, norm_bias):
    average = jnp.mean(values, axis=-1, keepdims=True)
    centred = values - average
    spread = jnp.mean(centred * centred, axis=-1, keepdims=True)
    inv_std = lax.rsqrt(spread + norm_eps)
    hat_vals = centred * inv_std
    return (
        hat_vals * norm_gain.astype(jnp.float32) + norm_bias.astype(jnp.float32),
        hat_vals,
        inv_std,
    )


def norm_back(incoming, hat_vals, inv_std, norm_gain):
    scaled = incoming * norm_gain.astype(jnp.float32)
    return inv_std * (
        scaled
        - jnp.mean(scaled, axis=-1, keepdims=True)
        - hat_vals * jnp.mean(scaled * hat_vals, axis=-1, keepdims=True)
    )


def forward_pass(params, layer_input, live):
    (
        first_gain,
        first_bias,
        qkv_weight,
        query_bias,
        value_bias,
        out_weight,
        out_bias,
        second_gain,
        second_bias,
        up_weight,
        up_bias,
        down_weight,
        down_bias,
    ) = params
    images, length, model_width = layer_input.shape
    head_count = model_width // HEAD_DIM
    score_scale = HEAD_DIM ** (-0.5)
    stream = layer_input.astype(jnp.float32)
    normed, first_hat, first_inv = layer_norm(stream, first_gain, first_bias)
    normed = normed.astype(jnp.bfloat16)
    projected = matmul(normed, qkv_weight)
    shape_heads = (images, length, head_count, HEAD_DIM)
    queries = (
        (projected[..., :model_width] + query_bias.astype(jnp.float32))
        .astype(jnp.bfloat16)
        .reshape(shape_heads)
    )
    key_rows = (
        projected[..., model_width : 2 * model_width].astype(jnp.bfloat16).reshape(shape_heads)
    )
    values = (
        (projected[..., 2 * model_width :] + value_bias.astype(jnp.float32))
        .astype(jnp.bfloat16)
        .reshape(shape_heads)
    )
    scores = batched("bqhd,bkhd->bhqk", queries, key_rows) * score_scale
    log_total = jnp.log(jnp.sum(jnp.exp(scores), axis=-1, keepdims=True))
    weights = jnp.exp(scores - log_total).astype(jnp.bfloat16)
    attended = (
        batched("bhqk,bkhd->bqhd", weights, values)
        .reshape(images, length, model_width)
        .astype(jnp.bfloat16)
    )
    middle = stream + matmul(attended, out_weight) + out_bias.astype(jnp.float32)
    second_normed, second_hat, second_inv = layer_norm(middle, second_gain, second_bias)
    second_normed = second_normed.astype(jnp.bfloat16)
    hidden_pre = matmul(second_normed, up_weight) + up_bias.astype(jnp.float32)
    normal_cdf = 0.5 * (1.0 + lax.erf(hidden_pre * root_half))
    hidden = (hidden_pre * normal_cdf).astype(jnp.bfloat16)
    result = middle + matmul(hidden, down_weight) + down_bias.astype(jnp.float32)
    image_mask = live.astype(jnp.float32)[:, None, None]
    output = (result * image_mask).astype(jnp.bfloat16)
    saved = (
        normed,
        first_hat,
        first_inv,
        queries,
        key_rows,
        values,
        log_total,
        attended,
        second_normed,
        second_hat,
        second_inv,
        hidden_pre,
        normal_cdf,
        hidden,
        image_mask,
    )
    return (output, saved)


def backward_pass(params, saved, cotangent):
    (
        first_gain,
        first_bias,
        qkv_weight,
        query_bias,
        value_bias,
        out_weight,
        out_bias,
        second_gain,
        second_bias,
        up_weight,
        up_bias,
        down_weight,
        down_bias,
    ) = params
    (
        normed,
        first_hat,
        first_inv,
        queries,
        key_rows,
        values,
        log_total,
        attended,
        second_normed,
        second_hat,
        second_inv,
        hidden_pre,
        normal_cdf,
        hidden,
        image_mask,
    ) = saved
    images, length, head_count, head_width = queries.shape
    flat_shape = (images, length, head_count * head_width)
    score_scale = HEAD_DIM ** (-0.5)
    upstream = cotangent.astype(jnp.float32) * image_mask
    upstream_low = upstream.astype(jnp.bfloat16)
    down_weight_grad = outer_product(hidden, upstream_low)
    down_bias_grad = jnp.sum(upstream, axis=(0, 1))
    hidden_grad = matmul(upstream_low, down_weight.T)
    density = jnp.exp(-0.5 * hidden_pre * hidden_pre) * density_coef
    pre_grad = hidden_grad * (normal_cdf + hidden_pre * density)
    pre_low = pre_grad.astype(jnp.bfloat16)
    up_weight_grad = outer_product(second_normed, pre_low)
    up_bias_grad = jnp.sum(pre_grad, axis=(0, 1))
    second_in = matmul(pre_low, up_weight.T)
    second_gain_grad = jnp.sum(second_in * second_hat, axis=(0, 1))
    second_bias_grad = jnp.sum(second_in, axis=(0, 1))
    middle_grad = upstream + norm_back(second_in, second_hat, second_inv, second_gain)
    middle_low = middle_grad.astype(jnp.bfloat16)
    out_weight_grad = outer_product(attended, middle_low)
    out_bias_grad = jnp.sum(middle_grad, axis=(0, 1))
    attended_grad = matmul(middle_low, out_weight.T).astype(jnp.bfloat16).reshape(queries.shape)
    again_scores = batched("bqhd,bkhd->bhqk", queries, key_rows) * score_scale
    probs = jnp.exp(again_scores - log_total)
    probs_low = probs.astype(jnp.bfloat16)
    value_grad = batched("bhqk,bqhd->bkhd", probs_low, attended_grad)
    prob_grad = batched("bqhd,bkhd->bhqk", attended_grad, values)
    score_grad = (
        probs * (prob_grad - jnp.sum(probs * prob_grad, axis=-1, keepdims=True)) * score_scale
    ).astype(jnp.bfloat16)
    query_grad = batched("bhqk,bkhd->bqhd", score_grad, key_rows).reshape(flat_shape)
    key_grad = batched("bhqk,bqhd->bkhd", score_grad, queries).reshape(flat_shape)
    value_grad = value_grad.reshape(flat_shape)
    joined = jnp.concatenate([query_grad, key_grad, value_grad], axis=-1).astype(jnp.bfloat16)
    qkv_weight_grad = outer_product(normed, joined)
    query_bias_grad = jnp.sum(query_grad, axis=(0, 1))
    value_bias_grad = jnp.sum(value_grad, axis=(0, 1))
    first_in = matmul(joined, qkv_weight.T)
    first_gain_grad = jnp.sum(first_in * first_hat, axis=(0, 1))
    first_bias_grad = jnp.sum(first_in, axis=(0, 1))
    middle_grad = middle_grad + norm_back(first_in, first_hat, first_inv, first_gain)
    input_grad = middle_grad.astype(jnp.bfloat16)
    grads = (
        first_gain_grad,
        first_bias_grad,
        qkv_weight_grad,
        query_bias_grad,
        value_bias_grad,
        out_weight_grad,
        out_bias_grad,
        second_gain_grad,
        second_bias_grad,
        up_weight_grad,
        up_bias_grad,
        down_weight_grad,
        down_bias_grad,
    )
    return (input_grad, grads)


def per_device(
    layer_input,
    cotangent,
    live,
    first_gain,
    first_bias,
    qkv_weight,
    query_bias,
    value_bias,
    out_weight,
    out_bias,
    second_gain,
    second_bias,
    up_weight,
    up_bias,
    down_weight,
    down_bias,
):
    gathered = (
        lax.all_gather(first_gain, "shard", axis=0, tiled=True),
        lax.all_gather(first_bias, "shard", axis=0, tiled=True),
        lax.all_gather(qkv_weight, "shard", axis=0, tiled=True),
        lax.all_gather(query_bias, "shard", axis=0, tiled=True),
        lax.all_gather(value_bias, "shard", axis=0, tiled=True),
        lax.all_gather(out_weight, "shard", axis=0, tiled=True),
        lax.all_gather(out_bias, "shard", axis=0, tiled=True),
        lax.all_gather(second_gain, "shard", axis=0, tiled=True),
        lax.all_gather(second_bias, "shard", axis=0, tiled=True),
        lax.all_gather(up_weight, "shard", axis=0, tiled=True),
        lax.all_gather(up_bias, "shard", axis=0, tiled=True),
        lax.all_gather(down_weight, "shard", axis=0, tiled=True),
        lax.all_gather(down_bias, "shard", axis=0, tiled=True),
    )
    output, saved = forward_pass(gathered, layer_input, live)
    backward_params = (
        lax.all_gather(first_gain, "shard", axis=0, tiled=True),
        lax.all_gather(first_bias, "shard", axis=0, tiled=True),
        lax.all_gather(qkv_weight, "shard", axis=0, tiled=True),
        lax.all_gather(query_bias, "shard", axis=0, tiled=True),
        lax.all_gather(value_bias, "shard", axis=0, tiled=True),
        lax.all_gather(out_weight, "shard", axis=0, tiled=True),
        lax.all_gather(out_bias, "shard", axis=0, tiled=True),
        lax.all_gather(second_gain, "shard", axis=0, tiled=True),
        lax.all_gather(second_bias, "shard", axis=0, tiled=True),
        lax.all_gather(up_weight, "shard", axis=0, tiled=True),
        lax.all_gather(up_bias, "shard", axis=0, tiled=True),
        lax.all_gather(down_weight, "shard", axis=0, tiled=True),
        lax.all_gather(down_bias, "shard", axis=0, tiled=True),
    )
    input_grad, grads = backward_pass(backward_params, saved, cotangent)
    g00, g01, g02, g03, g04, g05, g06, g07, g08, g09, g10, g11, g12 = grads
    owned = (
        lax.psum_scatter(g00, "shard", scatter_dimension=0, tiled=True),
        lax.psum_scatter(g01, "shard", scatter_dimension=0, tiled=True),
        lax.psum_scatter(g02, "shard", scatter_dimension=0, tiled=True),
        lax.psum_scatter(g03, "shard", scatter_dimension=0, tiled=True),
        lax.psum_scatter(g04, "shard", scatter_dimension=0, tiled=True),
        lax.psum_scatter(g05, "shard", scatter_dimension=0, tiled=True),
        lax.psum_scatter(g06, "shard", scatter_dimension=0, tiled=True),
        lax.psum_scatter(g07, "shard", scatter_dimension=0, tiled=True),
        lax.psum_scatter(g08, "shard", scatter_dimension=0, tiled=True),
        lax.psum_scatter(g09, "shard", scatter_dimension=0, tiled=True),
        lax.psum_scatter(g10, "shard", scatter_dimension=0, tiled=True),
        lax.psum_scatter(g11, "shard", scatter_dimension=0, tiled=True),
        lax.psum_scatter(g12, "shard", scatter_dimension=0, tiled=True),
    )
    o00, o01, o02, o03, o04, o05, o06, o07, o08, o09, o10, o11, o12 = owned
    quarter = (
        lax.psum_scatter(o00.astype(jnp.bfloat16), "rep", scatter_dimension=0, tiled=True).astype(
            jnp.float32
        ),
        lax.psum_scatter(o01.astype(jnp.bfloat16), "rep", scatter_dimension=0, tiled=True).astype(
            jnp.float32
        ),
        lax.psum_scatter(o02.astype(jnp.bfloat16), "rep", scatter_dimension=0, tiled=True).astype(
            jnp.float32
        ),
        lax.psum_scatter(o03.astype(jnp.bfloat16), "rep", scatter_dimension=0, tiled=True).astype(
            jnp.float32
        ),
        lax.psum_scatter(o04.astype(jnp.bfloat16), "rep", scatter_dimension=0, tiled=True).astype(
            jnp.float32
        ),
        lax.psum_scatter(o05.astype(jnp.bfloat16), "rep", scatter_dimension=0, tiled=True).astype(
            jnp.float32
        ),
        lax.psum_scatter(o06.astype(jnp.bfloat16), "rep", scatter_dimension=0, tiled=True).astype(
            jnp.float32
        ),
        lax.psum_scatter(o07.astype(jnp.bfloat16), "rep", scatter_dimension=0, tiled=True).astype(
            jnp.float32
        ),
        lax.psum_scatter(o08.astype(jnp.bfloat16), "rep", scatter_dimension=0, tiled=True).astype(
            jnp.float32
        ),
        lax.psum_scatter(o09.astype(jnp.bfloat16), "rep", scatter_dimension=0, tiled=True).astype(
            jnp.float32
        ),
        lax.psum_scatter(o10.astype(jnp.bfloat16), "rep", scatter_dimension=0, tiled=True).astype(
            jnp.float32
        ),
        lax.psum_scatter(o11.astype(jnp.bfloat16), "rep", scatter_dimension=0, tiled=True).astype(
            jnp.float32
        ),
        lax.psum_scatter(o12.astype(jnp.bfloat16), "rep", scatter_dimension=0, tiled=True).astype(
            jnp.float32
        ),
    )
    q00, q01, q02, q03, q04, q05, q06, q07, q08, q09, q10, q11, q12 = quarter
    summed = (
        lax.all_gather(q00.astype(jnp.bfloat16), "rep", axis=0, tiled=True).astype(q00.dtype),
        lax.all_gather(q01.astype(jnp.bfloat16), "rep", axis=0, tiled=True).astype(q01.dtype),
        lax.all_gather(q02.astype(jnp.bfloat16), "rep", axis=0, tiled=True).astype(q02.dtype),
        lax.all_gather(q03.astype(jnp.bfloat16), "rep", axis=0, tiled=True).astype(q03.dtype),
        lax.all_gather(q04.astype(jnp.bfloat16), "rep", axis=0, tiled=True).astype(q04.dtype),
        lax.all_gather(q05.astype(jnp.bfloat16), "rep", axis=0, tiled=True).astype(q05.dtype),
        lax.all_gather(q06.astype(jnp.bfloat16), "rep", axis=0, tiled=True).astype(q06.dtype),
        lax.all_gather(q07.astype(jnp.bfloat16), "rep", axis=0, tiled=True).astype(q07.dtype),
        lax.all_gather(q08.astype(jnp.bfloat16), "rep", axis=0, tiled=True).astype(q08.dtype),
        lax.all_gather(q09.astype(jnp.bfloat16), "rep", axis=0, tiled=True).astype(q09.dtype),
        lax.all_gather(q10.astype(jnp.bfloat16), "rep", axis=0, tiled=True).astype(q10.dtype),
        lax.all_gather(q11.astype(jnp.bfloat16), "rep", axis=0, tiled=True).astype(q11.dtype),
        lax.all_gather(q12.astype(jnp.bfloat16), "rep", axis=0, tiled=True).astype(q12.dtype),
    )
    return (
        output,
        input_grad,
        summed[0],
        summed[1],
        summed[2],
        summed[3],
        summed[4],
        summed[5],
        summed[6],
        summed[7],
        summed[8],
        summed[9],
        summed[10],
        summed[11],
        summed[12],
    )


def solution(mesh):
    placed = (
        P(("rep", "shard"), None, None),
        P(("rep", "shard"), None, None),
        P(("rep", "shard")),
        P("shard"),
        P("shard"),
        P("shard", None),
        P("shard"),
        P("shard"),
        P("shard", None),
        P("shard"),
        P("shard"),
        P("shard"),
        P("shard", None),
        P("shard"),
        P("shard", None),
        P("shard"),
    )
    return jax.shard_map(
        per_device,
        mesh=mesh,
        in_specs=placed,
        out_specs=(
            P(("rep", "shard"), None, None),
            P(("rep", "shard"), None, None),
            P("shard"),
            P("shard"),
            P("shard", None),
            P("shard"),
            P("shard"),
            P("shard", None),
            P("shard"),
            P("shard"),
            P("shard"),
            P("shard", None),
            P("shard"),
            P("shard", None),
            P("shard"),
        ),
        check_vma=False,
    )
```

profile of v0, /device:TPU:0, one launch (start us, length us, event | category | flops | bytes accessed | tf_op | source)
XLA Modules:
  0.0 931.1 jit_solution(7860005917995283044)
XLA Ops:
  10.0 1.3 fusion.110
  12.0 0.8 dynamic-update-slice.1
  12.9 0.8 dynamic-update-slice
  13.7 0.8 dynamic-update-slice.2
  14.6 0.8 dynamic-update-slice.3
  15.4 0.8 dynamic-update-slice.4
  16.2 0.8 dynamic-update-slice.7
  17.1 0.8 dynamic-update-slice.6
  17.9 0.8 dynamic-update-slice.5
  18.7 40.4 %all-reduce.36 = (bf16[768]{0:T(1024)(128)(2,1)S(1)}, bf16[768]{0:T(1024)(128)(2,1)S(1)}, bf16[768]{0:T(1024)(128)(2,1)S(1)}, bf16[768]{0:T(1024)(128)(2,1)S(1)}...) all-reduce(bf16[768]{0:T(1024)(128)(2,1)S(1)} %dynamic-update-slice, ...), channel_id=1, replica_groups=mesh['rep'=4,'shard'=8] {'shard'}, use_global_device_ids=true, to_apply=%add.1 | all-reduce | flops 6144 | bytes 24576
  60.5 26.5 %all-gather = bf16[8,1,384]{2,1,0:T(2,128)(2,1)S(1)} all-gather(bf16[1,1,384]{2,1,0:T(2,128)(2,1)S(1)} %reshape.374), channel_id=1, replica_groups=mesh['rep'=4,'shard'=8] {'shard'}, dimensions={0}, use_global_device_ids=true | all-gather | bytes 6912 | tf_op jit(solution)/shard_map/all_gather | solution.py:249
  87.0 1.1 convert_reduce_fusion
  88.4 3.0 convolution_bitcast_fusion
  91.4 0.8 slice.23
  92.2 0.9 copy.51
  93.1 0.9 copy.52
  94.0 1.1 copy.53
  95.2 1.7 fusion.118
  96.9 2.3 convolution_convert_fusion
  99.2 21.3 %all-gather.8.cloned.1.call-done = bf16[768,768]{1,0:T(8,128)(2,1)} async-done(((bf16[96,768]{1,0:T(8,128)(2,1)}), bf16[768,768]{1,0:T(8,128)(2,1)}) %all-gather.8.cloned.1.call-update) | async-done | bytes 1179664 | tf_op jit(solution)/shard_map/all_gather | solution.py:244
  120.5 1.8 fusion.112
  122.5 78.2 %all-gather.10.cloned.1.call-done = bf16[768,3072]{1,0:T(8,128)(2,1)} async-done(((bf16[96,3072]{1,0:T(8,128)(2,1)}), bf16[768,3072]{1,0:T(8,128)(2,1)}) %all-gather.10.cloned.1.call-update) | async-done | bytes 4718608 | tf_op jit(solution)/shard_map/all_gather | solution.py:248
  200.7 3.6 convolution_add_fusion
  204.3 76.2 %all-gather.12.cloned.1.call-done = bf16[3072,768]{1,0:T(8,128)(2,1)} async-done(((bf16[384,768]{1,0:T(8,128)(2,1)}), bf16[3072,768]{1,0:T(8,128)(2,1)}) %all-gather.12.cloned.1.call-update) | async-done | bytes 4718608 | tf_op jit(solution)/shard_map/all_gather | solution.py:250
  280.5 4.3 fusion.117
  284.9 1.8 fusion.52
  287.2 0.8 copy-done.1
  288.0 1.9 fusion.77
  290.2 3.9 fusion.6
  294.1 2.7 convolution_convert_fusion.1
  296.8 1.9 copy.55
  298.7 4.3 fusion.108
  303.0 3.1 fusion.119
  306.1 5.6 fusion.23
  311.7 5.5 fusion.109
  317.2 5.4 fusion.64
  322.7 6.5 fusion.56
  329.3 5.6 fusion.80
  335.0 23.1 %reduce-scatter.13.cloned.1.call-done = f32[96,768]{1,0:T(8,128)} async-done(((f32[768,768]{1,0:T(8,128)}), f32[96,768]{1,0:T(8,128)}) %reduce-scatter.13.cloned.1.call-update) | async-done | bytes 294928 | tf_op jit(solution)/shard_map/reduce_scatter | solution.py:277
  358.1 1.6 convert_element_type.249
  359.8 130.2 %reduce-scatter.9.cloned.1.call-done = f32[96,2304]{1,0:T(8,128)} async-done(((f32[768,2304]{1,0:T(8,128)}), f32[96,2304]{1,0:T(8,128)}) %reduce-scatter.9.cloned.1.call-update) | async-done | bytes 884752 | tf_op jit(solution)/shard_map/reduce_scatter | solution.py:274
  490.0 2.0 convert_element_type.243
  492.1 162.8 %reduce-scatter.17.cloned.1.call-done = f32[96,3072]{1,0:T(8,128)} async-done(((f32[768,3072]{1,0:T(8,128)}), f32[96,3072]{1,0:T(8,128)}) %reduce-scatter.17.cloned.1.call-update) | async-done | bytes 1179664 | tf_op jit(solution)/shard_map/reduce_scatter | solution.py:281
  654.9 2.2 convert_element_type.257
  661.1 3.8 fusion.48
  665.0 0.8 copy-done.3
  666.0 38.6 %all-reduce.35 = (bf16[768]{0:T(1024)(128)(2,1)S(1)}, bf16[768]{0:T(1024)(128)(2,1)S(1)}, bf16[768]{0:T(1024)(128)(2,1)S(1)}, bf16[768]{0:T(1024)(128)(2,1)S(1)}...) all-reduce(f32[768]{0:T(1024)S(1)} %get-tuple-element.17, ...), channel_id=2, replica_groups=mesh['rep'=4,'shard'=8] {'shard'}, use_global_device_ids=true, to_apply=%region_11.0.clone | all-reduce | flops 9216 | bytes 55296
  705.3 6.4 all-reduce.38
  714.2 6.7 all-reduce.37
  725.6 95.5 %reduce-scatter.21.cloned.1.call-done = f32[384,768]{1,0:T(8,128)} async-done(((f32[3072,768]{1,0:T(8,128)}), f32[384,768]{1,0:T(8,128)}) %reduce-scatter.21.cloned.1.call-update) | async-done | bytes 1179664 | tf_op jit(solution)/shard_map/reduce_scatter | solution.py:283
  821.1 2.2 convert_element_type.261
  823.3 2.2 fusion.47
  825.5 4.4 fusion.34
  829.9 13.0 %reduce-scatter.15.cloned.1.call-done = bf16[24,768]{1,0:T(8,128)(2,1)} async-done(((bf16[96,768]{1,0:T(8,128)(2,1)}), bf16[24,768]{1,0:T(8,128)(2,1)}) %reduce-scatter.15.cloned.1.call-update) | async-done | bytes 36880 | tf_op jit(solution)/shard_map/reduce_scatter | solution.py:303
  842.9 5.7 all_gather.102
  849.3 17.1 %reduce-scatter.11.cloned.1.call-done = bf16[24,2304]{1,0:T(8,128)(2,1)} async-done(((bf16[96,2304]{1,0:T(8,128)(2,1)}), bf16[24,2304]{1,0:T(8,128)(2,1)}) %reduce-scatter.11.cloned.1.call-update) | async-done | bytes 110608 | tf_op jit(solution)/shard_map/reduce_scatter | solution.py:294
  866.3 6.5 all_gather.99
  872.8 1.0 convert_element_type.244
  873.8 17.8 %reduce-scatter.19.cloned.1.call-done = bf16[24,3072]{1,0:T(8,128)(2,1)} async-done(((bf16[96,3072]{1,0:T(8,128)(2,1)}), bf16[24,3072]{1,0:T(8,128)(2,1)}) %reduce-scatter.19.cloned.1.call-update) | async-done | bytes 147472 | tf_op jit(solution)/shard_map/reduce_scatter | solution.py:315
  891.5 7.1 all_gather.106
  898.7 1.1 convert_element_type.258
  899.8 16.2 %reduce-scatter.23.cloned.1.call-done = bf16[96,768]{1,0:T(8,128)(2,1)} async-done(((bf16[384,768]{1,0:T(8,128)(2,1)}), bf16[96,768]{1,0:T(8,128)(2,1)}) %reduce-scatter.23.cloned.1.call-update) | async-done | bytes 147472 | tf_op jit(solution)/shard_map/reduce_scatter | solution.py:321
  916.0 7.1 all_gather.108
  923.1 1.1 convert_element_type.262
  (123 shorter events, 14.2 us)
Async XLA Ops:
  7.2 80.9 %copy-start = (bf16[1,197,768]{2,1,0:T(8,128)(2,1)S(1)}, bf16[1,197,768]{2,1,0:T(8,128)(2,1)}, u32[]{:S(2)}) copy-start(bf16[1,197,768]{2,1,0:T(8,128)(2,1)} %param.16) | copy-start | bytes 907780
  7.2 81.2 %all-gather.6.cloned.1.call-start = ((), (), s32[]{:S(2)}) async-start(), calls=%async_computation.8 | async-start | bytes 3981312 | tf_op jit(solution)/shard_map/all_gather | solution.py:241
  7.9 112.5 %all-gather.8.cloned.1.call-start = ((), (), s32[]{:S(2)}) async-start(), calls=%async_computation.9 | async-start | bytes 1327104 | tf_op jit(solution)/shard_map/all_gather | solution.py:244
  8.7 192.0 %all-gather.10.cloned.1.call-start = ((), (), s32[]{:S(2)}) async-start(), calls=%async_computation.10 | async-start | bytes 5308416 | tf_op jit(solution)/shard_map/all_gather | solution.py:248
  9.4 271.1 %all-gather.12.cloned.1.call-start = ((), (), s32[]{:S(2)}) async-start(), calls=%async_computation.11 | async-start | bytes 5308416 | tf_op jit(solution)/shard_map/all_gather | solution.py:250
  10.0 348.1 %reduce-scatter.13.cloned.1.call-start = ((), (), s32[]{:S(2)}) async-start(), calls=%async_computation.14 | async-start | bytes 2654208 | tf_op jit(solution)/shard_map/reduce_scatter | solution.py:277
  95.2 1.7 copy-start.7
  96.9 23.6 %copy-start.4 = (f32[12,197,197]{1,2,0:T(8,128)}, f32[12,197,197]{1,2,0:T(8,128)S(1)}, u32[]{:S(2)}) copy-start(f32[12,197,197]{1,2,0:T(8,128)S(1)} %fusion.118) | copy-start | bytes 5588500
  99.2 101.5 %copy-start.5 = (bf16[12,64,197]{2,1,0:T(8,128)(2,1)}, bf16[12,64,197]{2,1,0:T(8,128)(2,1)S(1)}, u32[]{:S(2)}) copy-start(bf16[12,64,197]{2,1,0:T(8,128)(2,1)S(1)} %convolution_convert_fusion) | copy-start | bytes 907780
  280.5 4.4 copy-start.2
  284.8 1.8 copy-start.9
  284.8 2.0 copy-start.8
  286.7 1.4 copy-start.6
  287.2 0.8 copy-start.1
  289.9 200.1 %reduce-scatter.9.cloned.1.call-start = ((), (), s32[]{:S(2)}) async-start(), calls=%async_computation.12 | async-start | bytes 7962624 | tf_op jit(solution)/shard_map/reduce_scatter | solution.py:274
  322.7 332.2 %reduce-scatter.17.cloned.1.call-start = ((), (), s32[]{:S(2)}) async-start(), calls=%async_computation.16 | async-start | bytes 10616832 | tf_op jit(solution)/shard_map/reduce_scatter | solution.py:281
  329.3 491.8 %reduce-scatter.21.cloned.1.call-start = ((), (), s32[]{:S(2)}) async-start(), calls=%async_computation.18 | async-start | bytes 10616832 | tf_op jit(solution)/shard_map/reduce_scatter | solution.py:283
  334.9 507.9 %reduce-scatter.15.cloned.1.call-start = ((), (), s32[]{:S(2)}) async-start(), calls=%async_computation.15 | async-start | bytes 184320 | tf_op jit(solution)/shard_map/reduce_scatter | solution.py:303
  359.8 506.6 %reduce-scatter.11.cloned.1.call-start = ((), (), s32[]{:S(2)}) async-start(), calls=%async_computation.13 | async-start | bytes 552960 | tf_op jit(solution)/shard_map/reduce_scatter | solution.py:294
  492.0 399.5 %reduce-scatter.19.cloned.1.call-start = ((), (), s32[]{:S(2)}) async-start(), calls=%async_computation.17 | async-start | bytes 737280 | tf_op jit(solution)/shard_map/reduce_scatter | solution.py:315
  657.1 258.9 %reduce-scatter.23.cloned.1.call-start = ((), (), s32[]{:S(2)}) async-start(), calls=%async_computation.19 | async-start | bytes 737280 | tf_op jit(solution)/shard_map/reduce_scatter | solution.py:321
  665.0 0.8 copy-start.3
Sparse Core Ops, SparseCore 0:
  10.2 68.0 all-gather.5
  80.4 39.9 all-gather.7
  122.7 78.0 all-gather.9
  202.7 77.6 all-gather.11
  290.0 68.0 reduce-scatter.12
  361.6 128.3 reduce-scatter.8
  493.6 161.2 reduce-scatter.16
  658.5 162.5 reduce-scatter.20
  824.1 18.7 reduce-scatter.14
  845.2 21.0 reduce-scatter.10
  869.4 22.0 reduce-scatter.18
  893.9 22.0 reduce-scatter.22
where the time goes:
time: 932 us; the launch traced here: 931 us
  waiting for transfers between devices  654 us (70%)
  blocking collectives  145 us (16%)
  matrix products  71.3 us (8%)
  other arithmetic  21.1 us (2%)
  between operations  19.7 us (2%)
  local copies, waits for them, and re-layouts  19.4 us (2%)
    reduce_scatter x1, waiting for transfers between devices, per_device(): lax.psum_scatter(g09, 'shard', scatter_dimension=0, tiled=True)  163 us
    reduce_scatter x1, waiting for transfers between devices, per_device(): lax.psum_scatter(g02, 'shard', scatter_dimension=0, tiled=True)  130 us
    reduce_scatter x1, waiting for transfers between devices, per_device(): lax.psum_scatter(g11, 'shard', scatter_dimension=0, tiled=True)  95.5 us
    unnamed x4, blocking collectives  92 us
    all_gather x1, waiting for transfers between devices, per_device(): lax.all_gather(up_weight, 'shard', axis=0, tiled=True)  78.2 us
    all_gather x1, waiting for transfers between devices, per_device(): lax.all_gather(down_weight, 'shard', axis=0, tiled=True)  76.2 us
    all_gather x1, blocking collectives, per_device(): lax.all_gather(up_bias, 'shard', axis=0, tiled=True)  26.5 us
    dot_general x8, matrix products, matmul(): product = jnp.dot(flat, factor, preferred_element_type=jnp.float32)  25.5 us
  transfers between devices with their start and end apart: 12, of which 11 were waited for; matrix products, arithmetic and copies ran while one was open for 11% of the time, Pallas kernels for 0%

commit v1 on v0

--- a/solution.py
+++ b/solution.py
@@ -1,6 +1,10 @@
+import functools
+
 import jax
 import jax.numpy as jnp
 from jax import lax
+from jax.experimental import pallas as pl
+from jax.experimental.pallas import tpu as pltpu
 from jax.sharding import PartitionSpec as P
 
 HEAD_DIM = 64
@@ -217,147 +221,419 @@
     return (input_grad, grads)
 
 
-def per_device(
-    layer_input,
-    cotangent,
-    live,
-    first_gain,
-    first_bias,
-    qkv_weight,
-    query_bias,
-    value_bias,
-    out_weight,
-    out_bias,
-    second_gain,
-    second_bias,
-    up_weight,
-    up_bias,
-    down_weight,
-    down_bias,
+MESH = pl.DeviceIdType.MESH
+UNIT = 16
+
+
+def ring_index(position, n):
+    half = position // (n // 2)
+    return (1 - half) * 2 * position + half * (2 * (n - 1 - position) + 1)
+
+
+def ring_position(index, n):
+    odd = index % 2
+    step = index // 2
+    return (1 - odd) * step + odd * (n - 1 - step)
+
+
+def make_streams(half_rows, n):
+    units = half_rows // UNIT
+    per_way = 2 if n <= 16 else 1
+    count = min(2 * per_way, units)
+    edges = [units * i // count for i in range(count + 1)]
+    return [
+        (1 if 2 * i < count else -1, edges[i] * UNIT, (edges[i + 1] - edges[i]) * UNIT)
+        for i in range(count)
+    ]
+
+
+def places(n):
+    rep = lax.axis_index("rep")
+    me = lax.axis_index("shard")
+    core = rep % 2
+    row = rep // 2
+    position = ring_position(me, n)
+    right = (rep, ring_index((position + 1) % n, n))
+    left = (rep, ring_index((position + n - 1) % n, n))
+    partner = (row * 2 + 1 - core, me)
+    across = ((1 - row) * 2 + core, me)
+    return me, core, row, position, right, left, partner, across
+
+
+def greet(peers):
+    barrier = pltpu.get_barrier_semaphore()
+    for peer in peers:
+        pl.semaphore_signal(barrier, inc=1, device_id=peer, device_id_type=MESH)
+    pl.semaphore_wait(barrier, len(peers))
+
+
+def remote(source, target, send, recv, device):
+    return pltpu.make_async_remote_copy(
+        src_ref=source,
+        dst_ref=target,
+        send_sem=send,
+        recv_sem=recv,
+        device_id=device,
+        device_id_type=MESH,
+    )
+
+
+def gather_kernel(
+    n,
+    half,
+    streams,
+    in_ref,
+    out_ref,
+    local_sem,
+    ring_s,
+    ring_r,
+    core_s,
+    core_r,
+    row_s,
+    row_r,
+    last_s,
+    last_r,
 ):
-    gathered = (
-        lax.all_gather(first_gain, "shard", axis=0, tiled=True),
-        lax.all_gather(first_bias, "shard", axis=0, tiled=True),
-        lax.all_gather(qkv_weight, "shard", axis=0, tiled=True),
-        lax.all_gather(query_bias, "shard", axis=0, tiled=True),
-        lax.all_gather(value_bias, "shard", axis=0, tiled=True),
-        lax.all_gather(out_weight, "shard", axis=0, tiled=True),
-        lax.all_gather(out_bias, "shard", axis=0, tiled=True),
-        lax.all_gather(second_gain, "shard", axis=0, tiled=True),
-        lax.all_gather(second_bias, "shard", axis=0, tiled=True),
-        lax.all_gather(up_weight, "shard", axis=0, tiled=True),
-        lax.all_gather(up_bias, "shard", axis=0, tiled=True),
-        lax.all_gather(down_weight, "shard", axis=0, tiled=True),
-        lax.all_gather(down_bias, "shard", axis=0, tiled=True),
-    )
+    me, core, row, position, right, left, partner, across = places(n)
+    own = pltpu.make_async_copy(in_ref, out_ref.at[me], local_sem)
+    own.start()
+    greet((right, left, partner, across))
+    own.wait()
+
+    def third(size):
+        return (size // UNIT // 3) * UNIT
+
+    def block(i, r):
+        sign = streams[i][0]
+        return ring_index((position + (n - sign) * r) % n, n)
+
+    def window(i, r, base, start, size):
+        first = pl.multiple_of(base * half + start, UNIT)
+        return out_ref.at[block(i, r), pl.ds(first, size)]
+
+    def ring(i, r):
+        sign, start, size = streams[i]
+        cut = third(size)
+        part = window(i, r, core, start + row * cut, size - cut)
+        return remote(part, part, ring_s.at[i, r], ring_r.at[i, r], right if sign > 0 else left)
+
+    def to_core(i, r, base):
+        sign, start, size = streams[i]
+        cut = third(size)
+        part = window(i, r + 1, base, start + row * cut, size - cut)
+        return remote(part, part, core_s.at[i, r], core_r.at[i, r], partner)
+
+    def to_row(i, r, which):
+        sign, start, size = streams[i]
+        cut = third(size)
+        part = window(i, r + 1, core, start + which * (size - cut), cut)
+        return remote(part, part, row_s.at[i, r], row_r.at[i, r], across)
+
+    def to_last(i, r, base):
+        sign, start, size = streams[i]
+        cut = third(size)
+        part = window(i, r + 1, base, start + (1 - row) * (size - cut), cut)
+        return remote(part, part, last_s.at[i, r], last_r.at[i, r], partner)
+
+    every = range(len(streams))
+    split = [i for i in every if third(streams[i][2]) > 0]
+
+    def arrived(i, r):
+        sign, start, size = streams[i]
+        cut = third(size)
+        part = window(i, r + 1, core, start + row * cut, size - cut)
+        return remote(part, part, ring_s.at[i, r], ring_r.at[i, r], right if sign > 0 else left)
+
+    for i in every:
+        ring(i, 0).start()
+
+    def relay(r):
+        for i in split:
+            to_row(i, r, 1 - row).wait_recv()
+            to_last(i, r, core).start()
+
+    def step(r, carry):
+        for i in every:
+            arrived(i, r).wait_recv()
+
+            @pl.when(r < n - 2)
+            def _():
+                ring(i, r + 1).start()
+
+            if third(streams[i][2]) > 0:
+                to_row(i, r, row).start()
+            to_core(i, r, core).start()
+
+        @pl.when(r > 0)
+        def _():
+            relay(r - 1)
+
+        return carry
+
+    lax.fori_loop(0, n - 1, step, 0)
+    relay(n - 2)
+
+    def finish(r, carry):
+        for i in every:
+            ring(i, r).wait_send()
+            to_core(i, r, core).wait_send()
+            to_core(i, r, 1 - core).wait_recv()
+        for i in split:
+            to_row(i, r, row).wait_send()
+            to_last(i, r, core).wait_send()
+            to_last(i, r, 1 - core).wait_recv()
+        return carry
+
+    lax.fori_loop(0, n - 1, finish, 0)
+
+
+def gather_all(packed, n):
+    rows, width = packed.shape
+    half = rows // 2
+    streams = make_streams(half, n)
+    sems = pltpu.SemaphoreType.DMA((len(streams), n - 1))
+    return pl.pallas_call(
+        functools.partial(gather_kernel, n, half, streams),
+        out_shape=jax.ShapeDtypeStruct((n, rows, width), packed.dtype),
+        in_specs=[pl.BlockSpec(memory_space=pltpu.VMEM)],
+        out_specs=pl.BlockSpec(memory_space=pl.ANY),
+        scratch_shapes=[pltpu.SemaphoreType.DMA] + [sems] * 8,
+        compiler_params=pltpu.CompilerParams(collective_id=0, has_side_effects=True),
+        name="gather_all",
+    )(packed)
+
+
+def reduce_kernel(
+    n,
+    half,
+    streams,
+    in_ref,
+    out_ref,
+    own,
+    given,
+    arrive,
+    other,
+    own_sem,
+    given_s,
+    given_r,
+    ring_s,
+    ring_r,
+    row_s,
+    row_r,
+    core_s,
+    core_r,
+):
+    me, core, row, position, right, left, partner, across = places(n)
+    every = range(len(streams))
+
+    def source(i, k, base):
+        sign, start, size = streams[i]
+        index = ring_index((position + (n - sign) * (k + 1)) % n, n)
+        first = pl.multiple_of(base * half + start, UNIT)
+        return in_ref.at[index, pl.ds(first, size)]
+
+    def part(ref, i, k):
+        sign, start, size = streams[i]
+        return ref.at[k, pl.ds(start, size)]
+
+    def load(i, k):
+        return pltpu.make_async_copy(source(i, k, core), part(own, i, k), own_sem.at[i, k])
+
+    def give(i, k):
+        return remote(
+            source(i, k, 1 - core), part(given, i, k), given_s.at[i, k], given_r.at[i, k], partner
+        )
+
+    def ring(i, k):
+        return remote(
+            part(own, i, k),
+            part(arrive, i, k),
+            ring_s.at[i, k],
+            ring_r.at[i, k],
+            right if streams[i][0] > 0 else left,
+        )
+
+    def loads(k, carry):
+        for i in every:
+            load(i, k).start()
+        return carry
+
+    lax.fori_loop(0, n, loads, 0)
+    greet((right, left, partner, across))
+
+    def gives(k, carry):
+        for i in every:
+            give(i, k).start()
+        return carry
+
+    lax.fori_loop(0, n, gives, 0)
+
+    def take(i, k):
+        load(i, k).wait()
+        give(i, k).wait_recv()
+        sign, start, size = streams[i]
+        rows = pl.ds(start, size)
+        return own[k, rows].astype(jnp.float32) + given[k, rows].astype(jnp.float32)
+
+    def put(i, k, total):
+        sign, start, size = streams[i]
+        own[k, pl.ds(start, size)] = total.astype(own.dtype)
+
+    for i in every:
+        put(i, 0, take(i, 0))
+        ring(i, 0).start()
+
+    def step(k, carry):
+        for i in every:
+            sign, start, size = streams[i]
+            total = take(i, k)
+            ring(i, k - 1).wait_recv()
+            put(i, k, total + arrive[k - 1, pl.ds(start, size)].astype(jnp.float32))
+            ring(i, k).start()
+        return carry
+
+    lax.fori_loop(1, n - 1, step, 0)
+
+    def to_row(i):
+        sign, start, size = streams[i]
+        return remote(
+            part(own, i, n - 1),
+            other.at[pl.ds(start, size)],
+            row_s.at[i],
+            row_r.at[i],
+            across,
+        )
+
+    def to_core(i, base):
+        sign, start, size = streams[i]
+        block = out_ref.at[base, pl.ds(start, size)]
+        return remote(block, block, core_s.at[i], core_r.at[i], partner)
+
+    for i in every:
+        sign, start, size = streams[i]
+        total = take(i, n - 1)
+        ring(i, n - 2).wait_recv()
+        put(i, n - 1, total + arrive[n - 2, pl.ds(start, size)].astype(jnp.float32))
+        to_row(i).start()
+    for i in every:
+        sign, start, size = streams[i]
+        rows = pl.ds(start, size)
+        to_row(i).wait_recv()
+        total = own[n - 1, rows].astype(jnp.float32) + other[rows].astype(jnp.float32)
+        out_ref[core, rows] = total.astype(out_ref.dtype)
+        to_core(i, core).start()
+    for i in every:
+        to_row(i).wait_send()
+        to_core(i, core).wait_send()
+        to_core(i, 1 - core).wait_recv()
+
+    def finish(k, carry):
+        for i in every:
+            give(i, k).wait_send()
+        return carry
+
+    lax.fori_loop(0, n, finish, 0)
+
+    def finish_ring(k, carry):
+        for i in every:
+            ring(i, k).wait_send()
+        return carry
+
+    lax.fori_loop(0, n - 1, finish_ring, 0)
+
+
+def reduce_all(blocks):
+    n, rows, width = blocks.shape
+    half = rows // 2
+    streams = make_streams(half, n)
+    count = len(streams)
+    dma = pltpu.SemaphoreType.DMA
+    low = blocks.dtype
+    return pl.pallas_call(
+        functools.partial(reduce_kernel, n, half, streams),
+        out_shape=jax.ShapeDtypeStruct((2, half, width), low),
+        in_specs=[pl.BlockSpec(memory_space=pl.ANY)],
+        out_specs=pl.BlockSpec(memory_space=pltpu.VMEM),
+        scratch_shapes=[
+            pltpu.VMEM((n, half, width), low),
+            pltpu.VMEM((n, half, width), low),
+            pltpu.VMEM((n - 1, half, width), low),
+            pltpu.VMEM((half, width), low),
+            dma((count, n)),
+            dma((count, n)),
+            dma((count, n)),
+            dma((count, n - 1)),
+            dma((count, n - 1)),
+            dma((count,)),
+            dma((count,)),
+            dma((count,)),
+            dma((count,)),
+        ],
+        compiler_params=pltpu.CompilerParams(
+            collective_id=1, has_side_effects=True, vmem_limit_bytes=48 * 1024 * 1024
+        ),
+        name="reduce_all",
+    )(blocks).reshape(rows, width)
+
+
+def per_device(n, layer_input, cotangent, live, *params):
+    width = params[0].shape[0] * n
+    matrices = [i for i, p in enumerate(params) if p.ndim == 2]
+    vectors = [i for i, p in enumerate(params) if p.ndim == 1]
+
+    pieces, place, row = [], {}, 0
+    for i in matrices:
+        rows, columns = params[i].shape
+        place[i] = []
+        for c in range(columns // width):
+            pieces.append(params[i][:, c * width : (c + 1) * width])
+            place[i].append(row)
+            row += rows
+    lengths = [params[i].shape[0] for i in vectors]
+    total = -(-(row * width + sum(lengths)) // (2 * UNIT * width)) * 2 * UNIT
+    spare = (total - row) * width - sum(lengths)
+    line = jnp.concatenate([params[i] for i in vectors] + [jnp.zeros(spare, params[0].dtype)])
+    pieces.append(line.reshape(total - row, width))
+    everything = gather_all(jnp.concatenate(pieces, axis=0), n)
+
+    gathered = [None] * len(params)
+    for i in matrices:
+        rows = params[i].shape[0]
+        gathered[i] = jnp.concatenate(
+            [everything[:, r : r + rows].reshape(n * rows, width) for r in place[i]], axis=1
+        )
+    tail = everything[:, row:].reshape(n, -1)
+    at = 0
+    for i, length in zip(vectors, lengths):
+        gathered[i] = tail[:, at : at + length].reshape(-1)
+        at += length
+
     output, saved = forward_pass(gathered, layer_input, live)
-    backward_params = (
-        lax.all_gather(first_gain, "shard", axis=0, tiled=True),
-        lax.all_gather(first_bias, "shard", axis=0, tiled=True),
-        lax.all_gather(qkv_weight, "shard", axis=0, tiled=True),
-        lax.all_gather(query_bias, "shard", axis=0, tiled=True),
-        lax.all_gather(value_bias, "shard", axis=0, tiled=True),
-        lax.all_gather(out_weight, "shard", axis=0, tiled=True),
-        lax.all_gather(out_bias, "shard", axis=0, tiled=True),
-        lax.all_gather(second_gain, "shard", axis=0, tiled=True),
-        lax.all_gather(second_bias, "shard", axis=0, tiled=True),
-        lax.all_gather(up_weight, "shard", axis=0, tiled=True),
-        lax.all_gather(up_bias, "shard", axis=0, tiled=True),
-        lax.all_gather(down_weight, "shard", axis=0, tiled=True),
-        lax.all_gather(down_bias, "shard", axis=0, tiled=True),
-    )
-    input_grad, grads = backward_pass(backward_params, saved, cotangent)
-    g00, g01, g02, g03, g04, g05, g06, g07, g08, g09, g10, g11, g12 = grads
-    owned = (
-        lax.psum_scatter(g00, "shard", scatter_dimension=0, tiled=True),
-        lax.psum_scatter(g01, "shard", scatter_dimension=0, tiled=True),
-        lax.psum_scatter(g02, "shard", scatter_dimension=0, tiled=True),
-        lax.psum_scatter(g03, "shard", scatter_dimension=0, tiled=True),
-        lax.psum_scatter(g04, "shard", scatter_dimension=0, tiled=True),
-        lax.psum_scatter(g05, "shard", scatter_dimension=0, tiled=True),
-        lax.psum_scatter(g06, "shard", scatter_dimension=0, tiled=True),
-        lax.psum_scatter(g07, "shard", scatter_dimension=0, tiled=True),
-        lax.psum_scatter(g08, "shard", scatter_dimension=0, tiled=True),
-        lax.psum_scatter(g09, "shard", scatter_dimension=0, tiled=True),
-        lax.psum_scatter(g10, "shard", scatter_dimension=0, tiled=True),
-        lax.psum_scatter(g11, "shard", scatter_dimension=0, tiled=True),
-        lax.psum_scatter(g12, "shard", scatter_dimension=0, tiled=True),
-    )
-    o00, o01, o02, o03, o04, o05, o06, o07, o08, o09, o10, o11, o12 = owned
-    quarter = (
-        lax.psum_scatter(o00.astype(jnp.bfloat16), "rep", scatter_dimension=0, tiled=True).astype(
+    input_grad, grads = backward_pass(gathered, saved, cotangent)
+
+    low = jnp.bfloat16
+    blocks = []
+    for i in matrices:
+        rows, columns = params[i].shape
+        grad = grads[i].astype(low)
+        for c in range(columns // width):
+            blocks.append(grad[:, c * width : (c + 1) * width].reshape(n, rows, width))
+    lines = [grads[i].astype(low).reshape(n, -1) for i in vectors] + [jnp.zeros((n, spare), low)]
+    blocks.append(jnp.concatenate(lines, axis=1).reshape(n, total - row, width))
+    summed = reduce_all(jnp.concatenate(blocks, axis=1))
+
+    results = [None] * len(params)
+    for i in matrices:
+        rows = params[i].shape[0]
+        results[i] = jnp.concatenate([summed[r : r + rows] for r in place[i]], axis=1).astype(
             jnp.float32
-        ),
-        lax.psum_scatter(o01.astype(jnp.bfloat16), "rep", scatter_dimension=0, tiled=True).astype(
-            jnp.float32
-        ),
-        lax.psum_scatter(o02.astype(jnp.bfloat16), "rep", scatter_dimension=0, tiled=True).astype(
-            jnp.float32
-        ),
-        lax.psum_scatter(o03.astype(jnp.bfloat16), "rep", scatter_dimension=0, tiled=True).astype(
-            jnp.float32
-        ),
-        lax.psum_scatter(o04.astype(jnp.bfloat16), "rep", scatter_dimension=0, tiled=True).astype(
-            jnp.float32
-        ),
-        lax.psum_scatter(o05.astype(jnp.bfloat16), "rep", scatter_dimension=0, tiled=True).astype(
-            jnp.float32
-        ),
-        lax.psum_scatter(o06.astype(jnp.bfloat16), "rep", scatter_dimension=0, tiled=True).astype(
-            jnp.float32
-        ),
-        lax.psum_scatter(o07.astype(jnp.bfloat16), "rep", scatter_dimension=0, tiled=True).astype(
-            jnp.float32
-        ),
-        lax.psum_scatter(o08.astype(jnp.bfloat16), "rep", scatter_dimension=0, tiled=True).astype(
-            jnp.float32
-        ),
-        lax.psum_scatter(o09.astype(jnp.bfloat16), "rep", scatter_dimension=0, tiled=True).astype(
-            jnp.float32
-        ),
-        lax.psum_scatter(o10.astype(jnp.bfloat16), "rep", scatter_dimension=0, tiled=True).astype(
-            jnp.float32
-        ),
-        lax.psum_scatter(o11.astype(jnp.bfloat16), "rep", scatter_dimension=0, tiled=True).astype(
-            jnp.float32
-        ),
-        lax.psum_scatter(o12.astype(jnp.bfloat16), "rep", scatter_dimension=0, tiled=True).astype(
-            jnp.float32
-        ),
-    )
-    q00, q01, q02, q03, q04, q05, q06, q07, q08, q09, q10, q11, q12 = quarter
-    summed = (
-        lax.all_gather(q00.astype(jnp.bfloat16), "rep", axis=0, tiled=True).astype(q00.dtype),
-        lax.all_gather(q01.astype(jnp.bfloat16), "rep", axis=0, tiled=True).astype(q01.dtype),
-        lax.all_gather(q02.astype(jnp.bfloat16), "rep", axis=0, tiled=True).astype(q02.dtype),
-        lax.all_gather(q03.astype(jnp.bfloat16), "rep", axis=0, tiled=True).astype(q03.dtype),
-        lax.all_gather(q04.astype(jnp.bfloat16), "rep", axis=0, tiled=True).astype(q04.dtype),
-        lax.all_gather(q05.astype(jnp.bfloat16), "rep", axis=0, tiled=True).astype(q05.dtype),
-        lax.all_gather(q06.astype(jnp.bfloat16), "rep", axis=0, tiled=True).astype(q06.dtype),
-        lax.all_gather(q07.astype(jnp.bfloat16), "rep", axis=0, tiled=True).astype(q07.dtype),
-        lax.all_gather(q08.astype(jnp.bfloat16), "rep", axis=0, tiled=True).astype(q08.dtype),
-        lax.all_gather(q09.astype(jnp.bfloat16), "rep", axis=0, tiled=True).astype(q09.dtype),
-        lax.all_gather(q10.astype(jnp.bfloat16), "rep", axis=0, tiled=True).astype(q10.dtype),
-        lax.all_gather(q11.astype(jnp.bfloat16), "rep", axis=0, tiled=True).astype(q11.dtype),
-        lax.all_gather(q12.astype(jnp.bfloat16), "rep", axis=0, tiled=True).astype(q12.dtype),
-    )
-    return (
-        output,
-        input_grad,
-        summed[0],
-        summed[1],
-        summed[2],
-        summed[3],
-        summed[4],
-        summed[5],
-        summed[6],
-        summed[7],
-        summed[8],
-        summed[9],
-        summed[10],
-        summed[11],
-        summed[12],
-    )
+        )
+    tail = summed[row:].reshape(-1)
+    at = 0
+    for i, length in zip(vectors, lengths):
+        results[i] = tail[at : at + length].astype(jnp.float32)
+        at += length
+    return (output, input_grad, *results)
 
 
 def solution(mesh):
@@ -380,7 +656,7 @@
         P("shard"),
     )
     return jax.shard_map(
-        per_device,
+        functools.partial(per_device, mesh.shape["shard"]),
         mesh=mesh,
         in_specs=placed,
         out_specs=(

time: 932 us -> 257 us (0.28)
  waiting for transfers between devices: 654 us -> 0 us
  Pallas kernels: 0 us -> 153 us
  blocking collectives: 145 us -> 0 us
  local copies, waits for them, and re-layouts: 19.4 us -> 38.8 us
  matrix products: 71.3 us -> 52.8 us
  between operations: 19.7 us -> 2.03 us
  other arithmetic: 21.1 us -> 9.43 us
    reduce_scatter x8 -> x0, waiting for transfers between devices: 476 us -> none  [the longest x1 163 us: per_device(): lax.psum_scatter(g09, 'shard', scatter_dimension=0, tiled=True)]
    all_gather x4 -> x0, waiting for transfers between devices: 176 us -> none  [the longest x1 78.2 us: per_device(): lax.all_gather(up_weight, 'shard', axis=0, tiled=True)]
    pallas_call x0 -> x2, Pallas kernels: none -> 153 us  [the longest x1 90.8 us: reduce_all(): pl.pallas_call(functools.partial(reduce_kernel, n, half, streams), out_sh...]
    unnamed x4 -> x0, blocking collectives: 92 us -> none
    all_gather x5 -> x0, blocking collectives: 52.9 us -> none  [the longest x1 26.5 us: per_device(): lax.all_gather(up_bias, 'shard', axis=0, tiled=True)]
    dot_general x4, matrix products: 19.5 us -> 4.85 us  [outer_product(): jnp.dot(operand.reshape(-1, operand.shape[-1]).T, factor.reshape(-1, fact...]
    slice x0 -> x5, local copies, waits for them, and re-layouts: none -> 12.5 us  [the longest x2 12 us: per_device(): everything[:, r:r + rows].reshape(n * rows, width)]
    convert_element_type x24 -> x5, other arithmetic: 16.6 us -> 4.44 us  [the longest x3 3.17 us: per_device(): jnp.concatenate([summed[r:r + rows] for r in place[i]], axis=1)]
  transfers between devices with their start and end apart: 12 -> 0, of which waited for: 11 -> 0; matrix products, arithmetic and copies ran while one was open for 11% -> 0% of each run, Pallas kernels for 0% -> 0%
where the time goes in v1:
time: 257 us; the launch traced here: 256 us
  Pallas kernels  153 us (60%)
  matrix products  52.8 us (21%)
  local copies, waits for them, and re-layouts  38.8 us (15%)
  other arithmetic  9.43 us (4%)
    pallas_call x1, Pallas kernels, reduce_all(): pl.pallas_call(functools.partial(reduce_kernel, n, half, streams), out_sh...  90.8 us
    pallas_call x1, Pallas kernels, gather_all(): pl.pallas_call(functools.partial(gather_kernel, n, half, streams), out_sh...  62.4 us
    dot_general x8, matrix products, matmul(): product = jnp.dot(flat, factor, preferred_element_type=jnp.float32)  23 us
    dot_general x6, matrix products, batched(): return jnp.einsum(form, operand, factor, preferred_element_type=jnp.float32)  22.3 us
    unnamed x94, local copies, waits for them, and re-layouts  19.8 us
    slice x2, local copies, waits for them, and re-layouts, per_device(): everything[:, r:r + rows].reshape(n * rows, width)  12 us

profile of v1, /device:TPU:0, one launch (start us, length us, event | category | flops | bytes accessed | tf_op | source)
XLA Modules:
  0.0 256.3 jit_solution(3327030362514098169)
XLA Ops:
  0.7 1.0 slice_dynamic-update-slice_fusion.6
  1.7 0.9 slice_dynamic-update-slice_fusion.5
  2.7 0.9 slice_dynamic-update-slice_fusion.4
  3.6 0.9 constant_dynamic-update-slice_fusion.2
  4.5 0.9 slice_dynamic-update-slice_fusion.3
  5.4 0.9 slice_dynamic-update-slice_fusion.2
  6.4 0.9 slice_dynamic-update-slice_fusion.1
  7.3 0.9 slice_dynamic-update-slice_fusion
  8.6 1.2 copy-done.5
  9.8 62.4 %gather_all.1 = bf16[8,1184,768]{2,1,0:T(8,128)(2,1)} custom-call(bf16[1184,768]{1,0:T(8,128)(2,1)} %copy-done.5), custom_call_target="tpu_custom_call" | custom-call | tf_op jit(solution)/shard_map/gather_all/pallas_call | solution.py:395
  72.2 1.0 slice_bitcast_fusion
  73.2 0.2 copy.55
  73.5 0.7 copy-done.24
  74.4 6.8 %fusion.107 = (bf16[8,96,768]{2,1,0:T(8,128)(2,1)}, bf16[8,96,768]{2,1,0:T(8,128)(2,1)}, bf16[8,96,768]{2,1,0:T(8,128)(2,1)}, bf16[8,96,768]{2,1,0:T(8,128)(2,1)...) fusion(bf16[8,1184,768]{2,1,0:T(8,128)(2,1)} %gather_all.1), kind=kLoop, calls=%fused_computation.164 | loop fusion | bytes 18874368 | tf_op jit(solution)/shard_map/slice | solution.py:603
  81.3 0.1 convert_reduce_fusion
  81.5 0.2 fusion.51
  81.7 3.0 %convolution_bitcast_fusion = f32[1,197,2304]{2,1,0:T(8,128)S(1)} fusion(bf16[768,768]{1,0:T(8,128)(2,1)} %bitcast.161, bf16[768,768]{1,0:T(8,128)(2,1)} %bitcast.163, bf16[768,768]{1,0:T(8,128)(2,1)} %bitcast.165, bf16[1,197,768]{2,1,0:T(8,128)(2,1)S(1)} %copy-done.1, f32[768]{0:T(1024)S(1)} %reshape.507, f32[768]{0:T(1024)S(1)} %reshape.506, ...), kind=kOutput, calls=%fused_computation.6 | convolution fusion | flops 708696576 | bytes 5664808 | tf_op jit(solution)/shard_map/dot_general | solution.py:20
  84.8 1.1 fusion.52
  85.9 0.2 copy-done.14
  86.1 1.1 copy.43
  87.2 1.3 copy.44
  88.5 1.2 slice.294
  89.8 0.2 copy.45
  90.0 2.0 fusion.119
  91.9 3.4 %convolution_convert_fusion.4 = bf16[12,64,197]{2,1,0:T(8,128)(2,1)S(1)} fusion(bf16[197,12,64]{0,2,1:T(8,128)(2,1)S(1)} %bitcast.148, f32[12,197,197]{1,2,0:T(8,128)} %fusion.119), kind=kOutput, calls=%fused_computation.34 | convolution fusion | flops 61627312 | bytes 2468016 | tf_op jit(solution)/shard_map/bhqk,bkhd->bqhd/dot_general | solution.py:33
  95.4 0.5 fusion.113
  95.9 0.8 slice_convert_fusion.3
  96.8 0.2 multiply_reduce_fusion.1
  97.1 5.3 %multiply_convert_fusion.1 = (bf16[197,3072]{1,0:T(8,128)(2,1)S(1)}, f32[197,3072]{1,0:T(8,128)}) fusion(f32[3072]{0:T(1024)S(1)} %reshape.513, bf16[768,768]{1,0:T(8,128)(2,1)} %bitcast.169, bf16[768,768]{1,0:T(8,128)(2,1)} %bitcast.171, bf16[768,768]{1,0:T(8,128)(2,1)} %bitcast.173, bf16[768,768]{1,0:T(8,128)(2,1)} %bitcast.167, ...), kind=kOutput, calls=%fused_computation.20 | convolution fusion | flops 952824576 | bytes 8974888 | tf_op jit(solution)/shard_map/dot_general | solution.py:20
  102.4 5.2 %slice.193 = bf16[8,384,768]{2,1,0:T(8,128)(2,1)} slice(bf16[8,1184,768]{2,1,0:T(8,128)(2,1)} %gather_all.1), slice={[0:8], [768:1152], [0:768]} | slice | bytes 9437184 | tf_op jit(solution)/shard_map/slice | solution.py:603
  108.4 4.4 %fusion.35 = bf16[1,197,768]{2,1,0:T(8,128)(2,1)} fusion(f32[1,197,768]{2,1,0:T(8,128)S(1)} %get-tuple-element.72, bf16[197,3072]{1,0:T(8,128)(2,1)S(1)} %get-tuple-element.73, bf16[3072,768]{1,0:T(8,128)(2,1)} %bitcast.145, f32[]{:T(128)} %bitcast.20, f32[768]{0:T(1024)S(1)} %reshape.514), kind=kOutput, calls=%fused_computation.43 | convolution fusion | flops 930167808 | bytes 6839812 | tf_op jit(solution)/shard_map/dot_general | solution.py:20
  112.8 3.7 %fusion.118 = (bf16[3072]{0:T(1024)(128)(2,1)S(1)}, bf16[197,3072]{1,0:T(8,128)(2,1)S(1)}) fusion(f32[197,3072]{1,0:T(8,128)} %get-tuple-element.74, bf16[3072,768]{1,0:T(8,128)(2,1)S(1)} %bitcast.146, bf16[1,197,768]{2,1,0:T(8,128)(2,1)S(1)} %copy-done.17, f32[]{:T(128)} %bitcast.20), kind=kOutput, calls=%fused_computation.171 | convolution fusion | flops 936670464 | bytes 8658436 | tf_op jit(solution)/shard_map/dot_general | solution.py:20
  116.6 1.8 fusion.54
  118.4 0.2 fusion.103
  118.5 0.3 fusion.105
  118.9 0.6 convolution_convert_fusion.5
  119.5 0.2 copy.47
  119.6 4.2 %fusion.111 = (bf16[12,64]{1,0:T(8,128)(2,1)S(1)}, bf16[1,197,12,64]{1,3,2,0:T(8,128)(2,1)}) fusion(bf16[197,12,64]{0,2,1:T(8,128)(2,1)S(1)} %bitcast.157, f32[12,197,197]{1,2,0:T(8,128)} %fusion.119), kind=kOutput, calls=%fused_computation.168 | convolution fusion | flops 61777840 | bytes 2469552 | tf_op jit(solution)/shard_map/bhqk,bqhd->bkhd/dot_general | solution.py:33
  123.8 2.6 %fusion.6 = f32[12,197,197]{1,2,0:T(8,128)} fusion(bf16[197,12,64]{0,2,1:T(8,128)(2,1)S(1)} %bitcast.151, bf16[197,12,64]{0,2,1:T(8,128)(2,1)S(1)} %bitcast.154), kind=kOutput, calls=%fused_computation.16 | convolution fusion | flops 120620928 | bytes 2468016 | tf_op jit(solution)/shard_map/reduce_sum | solution.py:96
  126.4 2.0 fusion.120
  128.4 5.4 %fusion.24 = bf16[12,64,197]{2,1,0:T(8,128)(2,1)} fusion(bf16[197,12,64]{0,2,1:T(8,128)(2,1)S(1)} %bitcast.152, f32[12,197,197]{1,2,0:T(8,128)} %fusion.6, f32[12,197,197]{1,2,0:T(8,128)} %fusion.120), kind=kOutput, calls=%fused_computation.33 | convolution fusion | flops 62093020 | bytes 4330848 | tf_op jit(solution)/shard_map/bhqk,bqhd->bkhd/dot_general | solution.py:33
  133.8 5.4 %fusion.112 = (bf16[12,64]{1,0:T(8,128)(2,1)S(1)}, bf16[1,197,12,64]{1,3,2,0:T(8,128)(2,1)}) fusion(bf16[197,12,64]{0,2,1:T(8,128)(2,1)S(1)} %bitcast.155, f32[12,197,197]{1,2,0:T(8,128)} %fusion.6, f32[12,197,197]{1,2,0:T(8,128)} %fusion.120), kind=kOutput, calls=%fused_computation.169 | convolution fusion | flops 62243548 | bytes 4332384 | tf_op jit(solution)/shard_map/bhqk,bkhd->bqhd/dot_general | solution.py:33
  139.2 3.7 %fusion.50 = (bf16[768]{0:T(1024)(128)(2,1)S(1)}, f32[197]{0:T(256)S(1)}, f32[197,768]{1,0:T(8,128)S(1)}) fusion(bf16[1,197,768]{2,1,0:T(8,128)(2,1)S(1)} %copy-done.1, f32[197]{0:T(256)S(1)} %add_rsqrt_fusion.1, f32[197]{0:T(256)S(1)} %broadcast_multiply_fusion.5, f32[768]{0:T(1024)S(1)} %reshape.506, bf16[768,768]{1,0:T(8,128)(2,1)} %bitcast.162, ...), kind=kOutput, calls=%fused_computation.62 | convolution fusion | flops 711721536 | bytes 5361468 | tf_op jit(solution)/shard_map/dot_general | solution.py:20
  142.9 0.2 fusion.104
  143.1 1.0 fusion.49
  144.1 1.3 convolution_convert_fusion.2
  145.4 0.2 fusion.109
  145.9 0.8 copy-done.13
  146.7 0.5 convolution_convert_fusion.3
  147.3 0.7 copy-done.16
  148.0 1.6 convolution_convert_fusion.1
  149.6 0.3 fusion.108
  150.3 1.1 copy-done.4
  151.4 1.5 convolution_convert_fusion
  152.9 0.3 constant_dynamic-update-slice_fusion.3
  153.3 5.2 %copy-done = bf16[8,1184,768]{2,1,0:T(8,128)(2,1)} copy-done((bf16[8,1184,768]{2,1,0:T(8,128)(2,1)}, bf16[8,1184,768]{2,1,0:T(8,128)(2,1)S(1)}, u32[]{:S(2)}) %copy-start) | copy-done | bytes 14549016
  159.3 0.8 bitcast_dynamic-update-slice_fusion.in_ref
  160.1 90.8 %reduce_all.1 = bf16[2,592,768]{2,1,0:T(8,128)(2,1)S(1)} custom-call(bf16[8,1184,768]{2,1,0:T(8,128)(2,1)} %bitcast_dynamic-update-slice_fusion.in_ref), custom_call_target="tpu_custom_call" | custom-call | tf_op jit(solution)/shard_map/reduce_all/pallas_call | solution.py:552
  251.0 0.6 slice_convert_fusion.13
  251.6 0.8 fusion.110
  252.4 1.0 maximum_convert_fusion.1
  253.4 1.1 maximum_convert_fusion
  254.5 0.6 slice_convert_fusion.12
  255.2 1.1 slice_convert_fusion.1
  (110 shorter events, 2.6 us)
Async XLA Ops:
  0.6 7.6 %copy-start.23 = (bf16[384,768]{1,0:T(8,128)(2,1)S(1)}, bf16[384,768]{1,0:T(8,128)(2,1)}, u32[]{:S(2)}) copy-start(bf16[384,768]{1,0:T(8,128)(2,1)} %param.30) | copy-start | bytes 1769476
  0.7 7.6 %copy-start.26 = (bf16[96]{0:T(256)(128)(2,1)S(1)}, bf16[96]{0:T(256)(128)(2,1)}, u32[]{:S(2)}) copy-start(bf16[96]{0:T(256)(128)(2,1)} %param.19) | copy-start | bytes 580
  0.7 7.6 %copy-start.27 = (bf16[96]{0:T(256)(128)(2,1)S(1)}, bf16[96]{0:T(256)(128)(2,1)}, u32[]{:S(2)}) copy-start(bf16[96]{0:T(256)(128)(2,1)} %param.20) | copy-start | bytes 580
  0.7 7.6 %copy-start.28 = (bf16[96]{0:T(256)(128)(2,1)S(1)}, bf16[96]{0:T(256)(128)(2,1)}, u32[]{:S(2)}) copy-start(bf16[96]{0:T(256)(128)(2,1)} %param.22) | copy-start | bytes 580
  0.7 7.6 %copy-start.29 = (bf16[96]{0:T(256)(128)(2,1)S(1)}, bf16[96]{0:T(256)(128)(2,1)}, u32[]{:S(2)}) copy-start(bf16[96]{0:T(256)(128)(2,1)} %param.23) | copy-start | bytes 580
  0.7 7.6 %copy-start.30 = (bf16[96]{0:T(256)(128)(2,1)S(1)}, bf16[96]{0:T(256)(128)(2,1)}, u32[]{:S(2)}) copy-start(bf16[96]{0:T(256)(128)(2,1)} %param.25) | copy-start | bytes 580
  0.7 7.6 %copy-start.31 = (bf16[96]{0:T(256)(128)(2,1)S(1)}, bf16[96]{0:T(256)(128)(2,1)}, u32[]{:S(2)}) copy-start(bf16[96]{0:T(256)(128)(2,1)} %param.26) | copy-start | bytes 580
  0.7 7.6 %copy-start.32 = (bf16[96]{0:T(256)(128)(2,1)S(1)}, bf16[96]{0:T(256)(128)(2,1)}, u32[]{:S(2)}) copy-start(bf16[96]{0:T(256)(128)(2,1)} %param.27) | copy-start | bytes 580
  0.7 7.6 %copy-start.25 = (bf16[384]{0:T(512)(128)(2,1)S(1)}, bf16[384]{0:T(512)(128)(2,1)}, u32[]{:S(2)}) copy-start(bf16[384]{0:T(512)(128)(2,1)} %param.29) | copy-start | bytes 2308
  0.7 7.6 %copy-start.33 = (bf16[96]{0:T(256)(128)(2,1)S(1)}, bf16[96]{0:T(256)(128)(2,1)}, u32[]{:S(2)}) copy-start(bf16[96]{0:T(256)(128)(2,1)} %param.31) | copy-start | bytes 580
  8.6 1.2 copy-start.5
  73.5 0.7 copy-start.24
  74.4 6.9 %copy-start.1 = (bf16[1,197,768]{2,1,0:T(8,128)(2,1)S(1)}, bf16[1,197,768]{2,1,0:T(8,128)(2,1)}, u32[]{:S(2)}) copy-start(bf16[1,197,768]{2,1,0:T(8,128)(2,1)} %param.16) | copy-start | bytes 907780
  84.7 1.4 copy-start.14
  87.2 4.7 %copy-start.6 = (bf16[1,197,768]{1,2,0:T(8,128)(2,1)}, bf16[1,197,768]{1,2,0:T(8,128)(2,1)S(1)}, u32[]{:S(2)}) copy-start(bf16[1,197,768]{1,2,0:T(8,128)(2,1)S(1)} %copy.43) | copy-start | bytes 907780
  88.5 6.8 %copy-start.8 = (bf16[1,197,768]{1,2,0:T(8,128)(2,1)}, bf16[1,197,768]{1,2,0:T(8,128)(2,1)S(1)}, u32[]{:S(2)}) copy-start(bf16[1,197,768]{1,2,0:T(8,128)(2,1)S(1)} %copy.44) | copy-start | bytes 907780
  90.0 5.4 %copy-start.10 = (bf16[1,197,768]{1,2,0:T(8,128)(2,1)}, bf16[1,197,768]{1,2,0:T(8,128)(2,1)S(1)}, u32[]{:S(2)}) copy-start(bf16[1,197,768]{1,2,0:T(8,128)(2,1)S(1)} %copy.45) | copy-start | bytes 907780
  95.4 1.7 copy-start.12
  102.4 5.9 %copy-start.3 = (bf16[197,3072]{1,0:T(8,128)(2,1)}, bf16[197,3072]{1,0:T(8,128)(2,1)S(1)}, u32[]{:S(2)}) copy-start(bf16[197,3072]{1,0:T(8,128)(2,1)S(1)} %get-tuple-element.73) | copy-start | bytes 3631108
  108.4 4.4 %copy-start.2 = (bf16[8,384,768]{2,1,0:T(8,128)(2,1)S(1)}, bf16[8,384,768]{2,1,0:T(8,128)(2,1)}, u32[]{:S(2)}) copy-start(bf16[8,384,768]{2,1,0:T(8,128)(2,1)} %slice.193) | copy-start | bytes 14155780
  108.4 4.4 %copy-start.17 = (bf16[1,197,768]{2,1,0:T(8,128)(2,1)S(1)}, bf16[1,197,768]{2,1,0:T(8,128)(2,1)}, u32[]{:S(2)}) copy-start(bf16[1,197,768]{2,1,0:T(8,128)(2,1)} %param.17) | copy-start | bytes 907780
  112.8 3.8 %copy-start.19 = (bf16[8,96,768]{2,1,0:T(8,128)(2,1)S(1)}, bf16[8,96,768]{2,1,0:T(8,128)(2,1)}, u32[]{:S(2)}) copy-start(bf16[8,96,768]{2,1,0:T(8,128)(2,1)} %get-tuple-element.25) | copy-start | bytes 3538948
  112.8 3.8 %copy-start.20 = (bf16[8,96,768]{2,1,0:T(8,128)(2,1)S(1)}, bf16[8,96,768]{2,1,0:T(8,128)(2,1)}, u32[]{:S(2)}) copy-start(bf16[8,96,768]{2,1,0:T(8,128)(2,1)} %get-tuple-element.26) | copy-start | bytes 3538948
  112.8 3.8 %copy-start.21 = (bf16[8,96,768]{2,1,0:T(8,128)(2,1)S(1)}, bf16[8,96,768]{2,1,0:T(8,128)(2,1)}, u32[]{:S(2)}) copy-start(bf16[8,96,768]{2,1,0:T(8,128)(2,1)} %get-tuple-element.27) | copy-start | bytes 3538948
  112.8 3.8 %copy-start.22 = (bf16[8,96,768]{2,1,0:T(8,128)(2,1)S(1)}, bf16[8,96,768]{2,1,0:T(8,128)(2,1)}, u32[]{:S(2)}) copy-start(bf16[8,96,768]{2,1,0:T(8,128)(2,1)} %get-tuple-element.28) | copy-start | bytes 3538948
  116.5 1.9 copy-start.15
  119.4 4.4 %copy-start.9 = (bf16[1,197,768]{1,2,0:T(8,128)(2,1)S(1)}, bf16[1,197,768]{1,2,0:T(8,128)(2,1)}, u32[]{:S(2)}) copy-start(bf16[1,197,768]{1,2,0:T(8,128)(2,1)} %copy-done.8) | copy-start | bytes 907780
  119.4 4.4 %copy-start.11 = (bf16[1,197,768]{1,2,0:T(8,128)(2,1)S(1)}, bf16[1,197,768]{1,2,0:T(8,128)(2,1)}, u32[]{:S(2)}) copy-start(bf16[1,197,768]{1,2,0:T(8,128)(2,1)} %copy-done.10) | copy-start | bytes 907780
  123.8 2.6 %copy-start.7 = (bf16[1,197,768]{1,2,0:T(8,128)(2,1)S(1)}, bf16[1,197,768]{1,2,0:T(8,128)(2,1)}, u32[]{:S(2)}) copy-start(bf16[1,197,768]{1,2,0:T(8,128)(2,1)} %copy-done.6) | copy-start | bytes 907780
  128.4 10.8 %copy-start.34 = (bf16[1,197,12,64]{1,3,2,0:T(8,128)(2,1)S(1)}, bf16[1,197,12,64]{1,3,2,0:T(8,128)(2,1)}, u32[]{:S(2)}) copy-start(bf16[1,197,12,64]{1,3,2,0:T(8,128)(2,1)} %get-tuple-element.51) | copy-start | bytes 907780
  142.9 1.2 copy-start.35
  142.9 1.2 copy-start.36
  145.7 1.0 copy-start.13
  146.7 1.3 copy-start.16
  150.1 1.3 copy-start.4
  150.1 1.3 copy-start.18
  153.3 5.2 %copy-start = (bf16[8,1184,768]{2,1,0:T(8,128)(2,1)}, bf16[8,1184,768]{2,1,0:T(8,128)(2,1)S(1)}, u32[]{:S(2)}) copy-start(bf16[8,1184,768]{2,1,0:T(8,128)(2,1)S(1)} %constant_dynamic-update-slice_fusion.3) | copy-start | bytes 43646980

commit v2 on v1

--- a/solution.py
+++ b/solution.py
@@ -222,9 +222,6 @@
 
 
 MESH = pl.DeviceIdType.MESH
-UNIT = 16
-
-
 def ring_index(position, n):
     half = position // (n // 2)
     return (1 - half) * 2 * position + half * (2 * (n - 1 - position) + 1)
@@ -234,17 +231,6 @@
     odd = index % 2
     step = index // 2
     return (1 - odd) * step + odd * (n - 1 - step)
-
-
-def make_streams(half_rows, n):
-    units = half_rows // UNIT
-    per_way = 2 if n <= 16 else 1
-    count = min(2 * per_way, units)
-    edges = [units * i // count for i in range(count + 1)]
-    return [
-        (1 if 2 * i < count else -1, edges[i] * UNIT, (edges[i + 1] - edges[i]) * UNIT)
-        for i in range(count)
-    ]
 
 
 def places(n):
@@ -278,12 +264,40 @@
     )
 
 
+def window(refs, side, part, block, width):
+    qkv, out, up, down = refs
+    if side == 2:
+        return [(None, down.at[block, part])]
+    if side == 1:
+        return [(None, up.at[block, :, pl.ds(pl.multiple_of(part * width, width), width)])]
+    inner = part - part // 3
+    return [
+        (part < 3, qkv.at[block, :, pl.ds(pl.multiple_of(inner * width, width), width)]),
+        (part == 3, out.at[block]),
+    ]
+
+
+def start_each(views, make):
+    for condition, view in views:
+        if condition is None:
+            make(view).start()
+        else:
+            pl.when(condition)(make(view).start)
+
+
 def gather_kernel(
     n,
-    half,
-    streams,
-    in_ref,
+    width,
+    qkv_in,
+    out_in,
+    up_in,
+    down_in,
+    line_in,
+    qkv_ref,
     out_ref,
+    up_ref,
+    down_ref,
+    line_ref,
     local_sem,
     ring_s,
     ring_r,
@@ -293,76 +307,79 @@
     row_r,
     last_s,
     last_r,
+    line_s,
+    line_r,
 ):
     me, core, row, position, right, left, partner, across = places(n)
-    own = pltpu.make_async_copy(in_ref, out_ref.at[me], local_sem)
-    own.start()
+    refs = (qkv_ref, out_ref, up_ref, down_ref)
+    pairs = zip((qkv_in, out_in, up_in, down_in, line_in), refs + (line_ref,))
+    locals_ = [
+        pltpu.make_async_copy(source, target.at[me], local_sem.at[i])
+        for i, (source, target) in enumerate(pairs)
+    ]
+    for copy in locals_:
+        copy.start()
     greet((right, left, partner, across))
-    own.wait()
-
-    def third(size):
-        return (size // UNIT // 3) * UNIT
-
-    def block(i, r):
-        sign = streams[i][0]
-        return ring_index((position + (n - sign) * r) % n, n)
-
-    def window(i, r, base, start, size):
-        first = pl.multiple_of(base * half + start, UNIT)
-        return out_ref.at[block(i, r), pl.ds(first, size)]
+    for copy in locals_:
+        copy.wait()
+
+    def block(way, r):
+        return ring_index((position + (1 if way else n - 1) * r) % n, n)
+
+    def views(i, r, whose):
+        way, kind = i // 2, i % 2
+        side, part = (2, 2 * whose + way) if kind else (way, 2 * whose + row)
+        return window(refs, side, part, block(way, r), width)
+
+    def over(way, r, whose):
+        return window(refs, way, 2 * whose + 1 - row, block(way, r), width)
 
     def ring(i, r):
-        sign, start, size = streams[i]
-        cut = third(size)
-        part = window(i, r, core, start + row * cut, size - cut)
-        return remote(part, part, ring_s.at[i, r], ring_r.at[i, r], right if sign > 0 else left)
-
-    def to_core(i, r, base):
-        sign, start, size = streams[i]
-        cut = third(size)
-        part = window(i, r + 1, base, start + row * cut, size - cut)
-        return remote(part, part, core_s.at[i, r], core_r.at[i, r], partner)
-
-    def to_row(i, r, which):
-        sign, start, size = streams[i]
-        cut = third(size)
-        part = window(i, r + 1, core, start + which * (size - cut), cut)
-        return remote(part, part, row_s.at[i, r], row_r.at[i, r], across)
-
-    def to_last(i, r, base):
-        sign, start, size = streams[i]
-        cut = third(size)
-        part = window(i, r + 1, base, start + (1 - row) * (size - cut), cut)
-        return remote(part, part, last_s.at[i, r], last_r.at[i, r], partner)
-
-    every = range(len(streams))
-    split = [i for i in every if third(streams[i][2]) > 0]
-
-    def arrived(i, r):
-        sign, start, size = streams[i]
-        cut = third(size)
-        part = window(i, r + 1, core, start + row * cut, size - cut)
-        return remote(part, part, ring_s.at[i, r], ring_r.at[i, r], right if sign > 0 else left)
-
-    for i in every:
-        ring(i, 0).start()
+        peer = left if i // 2 else right
+        return lambda v: remote(v, v, ring_s.at[i, r], ring_r.at[i, r], peer)
+
+    def to_core(i, r):
+        return lambda v: remote(v, v, core_s.at[i, r], core_r.at[i, r], partner)
+
+    def to_row(way, r):
+        return lambda v: remote(v, v, row_s.at[way, r], row_r.at[way, r], across)
+
+    def to_last(way, r):
+        return lambda v: remote(v, v, last_s.at[way, r], last_r.at[way, r], partner)
+
+    def line(r):
+        view = line_ref.at[block(0, r)]
+        return remote(view, view, line_s.at[r], line_r.at[r], right)
+
+    def one(vs):
+        return vs[0][1]
+
+    for i in range(4):
+        start_each(views(i, 0, core), ring(i, 0))
+    line(0).start()
 
     def relay(r):
-        for i in split:
-            to_row(i, r, 1 - row).wait_recv()
-            to_last(i, r, core).start()
+        for way in range(2):
+            to_row(way, r)(one(over(way, r + 1, core))).wait_recv()
+            start_each(over(way, r + 1, core), to_last(way, r))
 
     def step(r, carry):
-        for i in every:
-            arrived(i, r).wait_recv()
+        for i in (0, 2, 1, 3):
+            got = views(i, r + 1, core)
+            ring(i, r)(one(got)).wait_recv()
 
             @pl.when(r < n - 2)
             def _():
-                ring(i, r + 1).start()
-
-            if third(streams[i][2]) > 0:
-                to_row(i, r, row).start()
-            to_core(i, r, core).start()
+                start_each(got, ring(i, r + 1))
+
+            if i % 2 == 0:
+                start_each(got, to_row(i // 2, r))
+            start_each(got, to_core(i, r))
+        line(r).wait_recv()
+
+        @pl.when(r < n - 2)
+        def _():
+            line(r + 1).start()
 
         @pl.when(r > 0)
         def _():
@@ -374,45 +391,56 @@
     relay(n - 2)
 
     def finish(r, carry):
-        for i in every:
-            ring(i, r).wait_send()
-            to_core(i, r, core).wait_send()
-            to_core(i, r, 1 - core).wait_recv()
-        for i in split:
-            to_row(i, r, row).wait_send()
-            to_last(i, r, core).wait_send()
-            to_last(i, r, 1 - core).wait_recv()
+        for i in range(4):
+            view = one(views(i, r, core))
+            ring(i, r)(view).wait_send()
+            to_core(i, r)(view).wait_send()
+            to_core(i, r)(view).wait_recv()
+        for way in range(2):
+            view = one(views(2 * way, r, core))
+            to_row(way, r)(view).wait_send()
+            to_last(way, r)(view).wait_send()
+            to_last(way, r)(view).wait_recv()
+        line(r).wait_send()
         return carry
 
     lax.fori_loop(0, n - 1, finish, 0)
 
 
-def gather_all(packed, n):
-    rows, width = packed.shape
-    half = rows // 2
-    streams = make_streams(half, n)
-    sems = pltpu.SemaphoreType.DMA((len(streams), n - 1))
+def gather_all(arrays, n, width):
+    dma = pltpu.SemaphoreType.DMA
     return pl.pallas_call(
-        functools.partial(gather_kernel, n, half, streams),
-        out_shape=jax.ShapeDtypeStruct((n, rows, width), packed.dtype),
-        in_specs=[pl.BlockSpec(memory_space=pltpu.VMEM)],
-        out_specs=pl.BlockSpec(memory_space=pl.ANY),
-        scratch_shapes=[pltpu.SemaphoreType.DMA] + [sems] * 8,
+        functools.partial(gather_kernel, n, width),
+        out_shape=[jax.ShapeDtypeStruct((n,) + a.shape, a.dtype) for a in arrays],
+        in_specs=[pl.BlockSpec(memory_space=pltpu.VMEM)] * len(arrays),
+        out_specs=[pl.BlockSpec(memory_space=pl.ANY)] * len(arrays),
+        scratch_shapes=[dma((len(arrays),))]
+        + [dma((4, n - 1))] * 4
+        + [dma((2, n - 1))] * 4
+        + [dma((n - 1,))] * 2,
         compiler_params=pltpu.CompilerParams(collective_id=0, has_side_effects=True),
         name="gather_all",
-    )(packed)
+    )(*arrays)
 
 
 def reduce_kernel(
     n,
-    half,
-    streams,
-    in_ref,
+    width,
+    qkv_ref,
     out_ref,
+    up_ref,
+    down_ref,
+    line_ref,
+    sums,
+    line_out,
     own,
     given,
     arrive,
+    over,
     other,
+    line_send,
+    line_got,
+    line_pair,
     own_sem,
     given_s,
     given_r,
@@ -420,189 +448,242 @@
     ring_r,
     row_s,
     row_r,
-    core_s,
-    core_r,
+    end_row_s,
+    end_row_r,
+    end_core_s,
+    end_core_r,
+    line_s,
+    line_r,
+    pair_s,
+    pair_r,
 ):
     me, core, row, position, right, left, partner, across = places(n)
-    every = range(len(streams))
-
-    def source(i, k, base):
-        sign, start, size = streams[i]
-        index = ring_index((position + (n - sign) * (k + 1)) % n, n)
-        first = pl.multiple_of(base * half + start, UNIT)
-        return in_ref.at[index, pl.ds(first, size)]
-
-    def part(ref, i, k):
-        sign, start, size = streams[i]
-        return ref.at[k, pl.ds(start, size)]
+    refs = (qkv_ref, out_ref, up_ref, down_ref)
+    f32 = jnp.float32
+
+    def block(way, k):
+        return ring_index((position + (1 if way else n - 1) * (k + 1)) % n, n)
+
+    def source(i, k, whose):
+        way, kind = i % 2, i // 2
+        side, part = (
+            (way, 2 * whose + row),
+            (2, 2 * whose + way),
+            (way, 2 * whose + 1 - row),
+        )[kind]
+        return window(refs, side, part, block(way, k), width)
 
     def load(i, k):
-        return pltpu.make_async_copy(source(i, k, core), part(own, i, k), own_sem.at[i, k])
+        return lambda v: pltpu.make_async_copy(v, own.at[i, k], own_sem.at[i, k])
 
     def give(i, k):
+        return lambda v: remote(v, given.at[i, k], given_s.at[i, k], given_r.at[i, k], partner)
+
+    def ring(i, k):
+        peer = left if i % 2 else right
+        return remote(own.at[i, k], arrive.at[i, k], ring_s.at[i, k], ring_r.at[i, k], peer)
+
+    def to_row(way, k):
         return remote(
-            source(i, k, 1 - core), part(given, i, k), given_s.at[i, k], given_r.at[i, k], partner
+            own.at[4 + way, k], over.at[way, k], row_s.at[way, k], row_r.at[way, k], across
         )
 
-    def ring(i, k):
-        return remote(
-            part(own, i, k),
-            part(arrive, i, k),
-            ring_s.at[i, k],
-            ring_r.at[i, k],
-            right if streams[i][0] > 0 else left,
-        )
+    def line_ring(k):
+        return remote(line_send.at[k], line_got.at[k], line_s.at[k], line_r.at[k], right)
+
+    order = (4, 5, 2, 3, 0, 1)
 
     def loads(k, carry):
-        for i in every:
-            load(i, k).start()
+        for i in order:
+            start_each(source(i, k, core), load(i, k))
         return carry
 
     lax.fori_loop(0, n, loads, 0)
     greet((right, left, partner, across))
 
     def gives(k, carry):
-        for i in every:
-            give(i, k).start()
+        for i in order:
+            start_each(source(i, k, 1 - core), give(i, k))
         return carry
 
     lax.fori_loop(0, n, gives, 0)
 
     def take(i, k):
-        load(i, k).wait()
-        give(i, k).wait_recv()
-        sign, start, size = streams[i]
-        rows = pl.ds(start, size)
-        return own[k, rows].astype(jnp.float32) + given[k, rows].astype(jnp.float32)
+        view = source(i, k, core)[0][1]
+        load(i, k)(view).wait()
+        give(i, k)(view).wait_recv()
+        return own[i, k].astype(f32) + given[i, k].astype(f32)
 
     def put(i, k, total):
-        sign, start, size = streams[i]
-        own[k, pl.ds(start, size)] = total.astype(own.dtype)
-
-    for i in every:
-        put(i, 0, take(i, 0))
+        own[i, k] = total.astype(own.dtype)
+
+    def ahead(k):
+        for way in range(2):
+            put(4 + way, k, take(4 + way, k))
+            to_row(way, k).start()
+
+    def partial(i, k, first):
+        total = take(i, k)
+        if i < 2:
+            to_row(i, k).wait_recv()
+            total = total + over[i, k].astype(f32)
+        if not first:
+            ring(i, k - 1).wait_recv()
+            total = total + arrive[i, k - 1].astype(f32)
+        return total
+
+    ahead(0)
+    line_send[0] = line_ref[block(0, 0)]
+    line_ring(0).start()
+    ahead(1)
+    for i in (2, 3, 0, 1):
+        put(i, 0, partial(i, 0, True))
         ring(i, 0).start()
 
     def step(k, carry):
-        for i in every:
-            sign, start, size = streams[i]
-            total = take(i, k)
-            ring(i, k - 1).wait_recv()
-            put(i, k, total + arrive[k - 1, pl.ds(start, size)].astype(jnp.float32))
+        ahead(k + 1)
+        for i in (2, 3, 0, 1):
+            put(i, k, partial(i, k, False))
             ring(i, k).start()
+        line_ring(k - 1).wait_recv()
+        line_send[k] = line_ref[block(0, k)] + line_got[k - 1]
+        line_ring(k).start()
         return carry
 
     lax.fori_loop(1, n - 1, step, 0)
 
-    def to_row(i):
-        sign, start, size = streams[i]
+    def end_row(i, k=None):
+        if i < 2:
+            view = sums.at[i, 2 * core + row]
+            return remote(view, view, end_row_s.at[i], end_row_r.at[i], across)
         return remote(
-            part(own, i, n - 1),
-            other.at[pl.ds(start, size)],
-            row_s.at[i],
-            row_r.at[i],
-            across,
+            own.at[i, n - 1], other.at[i - 2], end_row_s.at[i], end_row_r.at[i], across
         )
 
-    def to_core(i, base):
-        sign, start, size = streams[i]
-        block = out_ref.at[base, pl.ds(start, size)]
-        return remote(block, block, core_s.at[i], core_r.at[i], partner)
-
-    for i in every:
-        sign, start, size = streams[i]
-        total = take(i, n - 1)
-        ring(i, n - 2).wait_recv()
-        put(i, n - 1, total + arrive[n - 2, pl.ds(start, size)].astype(jnp.float32))
-        to_row(i).start()
-    for i in every:
-        sign, start, size = streams[i]
-        rows = pl.ds(start, size)
-        to_row(i).wait_recv()
-        total = own[n - 1, rows].astype(jnp.float32) + other[rows].astype(jnp.float32)
-        out_ref[core, rows] = total.astype(out_ref.dtype)
-        to_core(i, core).start()
-    for i in every:
-        to_row(i).wait_send()
-        to_core(i, core).wait_send()
-        to_core(i, 1 - core).wait_recv()
+    def end_core(j, side, part):
+        view = sums.at[side, part]
+        return remote(view, view, end_core_s.at[j], end_core_r.at[j], partner)
+
+    for i in (2, 3):
+        put(i, n - 1, partial(i, n - 1, False))
+        end_row(i).start()
+    line_ring(n - 2).wait_recv()
+    line_pair[0] = line_ref[me] + line_got[n - 2]
+    pair_row = remote(line_pair.at[0], line_pair.at[1], pair_s.at[0], pair_r.at[0], across)
+    pair_row.start()
+    for way in (0, 1):
+        sums[way, 2 * core + row] = partial(way, n - 1, False).astype(sums.dtype)
+        end_row(way).start()
+        end_core(way, way, 2 * core + row).start()
+    pair_row.wait()
+    line_pair[2] = line_pair[0] + line_pair[1]
+    pair_core = remote(line_pair.at[2], line_pair.at[3], pair_s.at[1], pair_r.at[1], partner)
+    pair_core.start()
+    for way in (0, 1):
+        end_row(2 + way).wait_recv()
+        total = own[2 + way, n - 1].astype(f32) + other[way].astype(f32)
+        sums[2, 2 * core + way] = total.astype(sums.dtype)
+        end_core(2 + way, 2, 2 * core + way).start()
+    for way in (0, 1):
+        end_row(way).wait_recv()
+        end_core(4 + way, way, 2 * core + 1 - row).start()
+    pair_core.wait()
+    line_out[...] = line_pair[2] + line_pair[3]
+    for i in range(4):
+        end_row(i).wait_send()
+    for j in range(6):
+        copy = end_core(j, 0, 0)
+        copy.wait_send()
+        copy.wait_recv()
 
     def finish(k, carry):
-        for i in every:
-            give(i, k).wait_send()
+        for i in range(6):
+            give(i, k)(source(i, k, core)[0][1]).wait_send()
+        for way in range(2):
+            to_row(way, k).wait_send()
         return carry
 
     lax.fori_loop(0, n, finish, 0)
 
     def finish_ring(k, carry):
-        for i in every:
+        for i in range(4):
             ring(i, k).wait_send()
+        line_ring(k).wait_send()
         return carry
 
     lax.fori_loop(0, n - 1, finish_ring, 0)
 
 
-def reduce_all(blocks):
-    n, rows, width = blocks.shape
-    half = rows // 2
-    streams = make_streams(half, n)
-    count = len(streams)
+def reduce_all(arrays, n, width):
     dma = pltpu.SemaphoreType.DMA
-    low = blocks.dtype
+    vmem = pltpu.VMEM
+    rows = arrays[0].shape[1]
+    low = arrays[0].dtype
+    line = arrays[-1].shape[1:]
+    anywhere = pl.BlockSpec(memory_space=pl.ANY)
+    near = pl.BlockSpec(memory_space=pltpu.VMEM)
     return pl.pallas_call(
-        functools.partial(reduce_kernel, n, half, streams),
-        out_shape=jax.ShapeDtypeStruct((2, half, width), low),
-        in_specs=[pl.BlockSpec(memory_space=pl.ANY)],
-        out_specs=pl.BlockSpec(memory_space=pltpu.VMEM),
+        functools.partial(reduce_kernel, n, width),
+        out_shape=[
+            jax.ShapeDtypeStruct((3, 4, rows, width), low),
+            jax.ShapeDtypeStruct(line, jnp.float32),
+        ],
+        in_specs=[anywhere] * 4 + [near],
+        out_specs=[near, near],
         scratch_shapes=[
-            pltpu.VMEM((n, half, width), low),
-            pltpu.VMEM((n, half, width), low),
-            pltpu.VMEM((n - 1, half, width), low),
-            pltpu.VMEM((half, width), low),
-            dma((count, n)),
-            dma((count, n)),
-            dma((count, n)),
-            dma((count, n - 1)),
-            dma((count, n - 1)),
-            dma((count,)),
-            dma((count,)),
-            dma((count,)),
-            dma((count,)),
+            vmem((6, n, rows, width), low),
+            vmem((6, n, rows, width), low),
+            vmem((4, n - 1, rows, width), low),
+            vmem((2, n, rows, width), low),
+            vmem((2, rows, width), low),
+            vmem((n - 1,) + line, jnp.float32),
+            vmem((n - 1,) + line, jnp.float32),
+            vmem((4,) + line, jnp.float32),
+            dma((6, n)),
+            dma((6, n)),
+            dma((6, n)),
+            dma((4, n - 1)),
+            dma((4, n - 1)),
+            dma((2, n)),
+            dma((2, n)),
+            dma((4,)),
+            dma((4,)),
+            dma((6,)),
+            dma((6,)),
+            dma((n - 1,)),
+            dma((n - 1,)),
+            dma((2,)),
+            dma((2,)),
         ],
         compiler_params=pltpu.CompilerParams(
-            collective_id=1, has_side_effects=True, vmem_limit_bytes=48 * 1024 * 1024
+            collective_id=1, has_side_effects=True, vmem_limit_bytes=56 * 1024 * 1024
         ),
         name="reduce_all",
-    )(blocks).reshape(rows, width)
+    )(*arrays)
+
+
+LANES = 128
 
 
 def per_device(n, layer_input, cotangent, live, *params):
     width = params[0].shape[0] * n
+    rows = params[0].shape[0]
     matrices = [i for i, p in enumerate(params) if p.ndim == 2]
     vectors = [i for i, p in enumerate(params) if p.ndim == 1]
-
-    pieces, place, row = [], {}, 0
-    for i in matrices:
-        rows, columns = params[i].shape
-        place[i] = []
-        for c in range(columns // width):
-            pieces.append(params[i][:, c * width : (c + 1) * width])
-            place[i].append(row)
-            row += rows
+    shapes = [params[i].shape for i in matrices]
+    assert shapes == [(rows, 3 * width), (rows, width), (rows, 4 * width), (4 * rows, width)]
     lengths = [params[i].shape[0] for i in vectors]
-    total = -(-(row * width + sum(lengths)) // (2 * UNIT * width)) * 2 * UNIT
-    spare = (total - row) * width - sum(lengths)
+    tall = -(-sum(lengths) // (16 * LANES)) * 16
+    spare = tall * LANES - sum(lengths)
+
     line = jnp.concatenate([params[i] for i in vectors] + [jnp.zeros(spare, params[0].dtype)])
-    pieces.append(line.reshape(total - row, width))
-    everything = gather_all(jnp.concatenate(pieces, axis=0), n)
-
+    sent = [params[i] for i in matrices]
+    sent[3] = sent[3].reshape(4, rows, width)
+    *full, lines = gather_all(sent + [line.reshape(tall, LANES)], n, width)
     gathered = [None] * len(params)
-    for i in matrices:
-        rows = params[i].shape[0]
-        gathered[i] = jnp.concatenate(
-            [everything[:, r : r + rows].reshape(n * rows, width) for r in place[i]], axis=1
-        )
-    tail = everything[:, row:].reshape(n, -1)
+    for i, array in zip(matrices, full):
+        gathered[i] = array.reshape(n * params[i].shape[0], params[i].shape[1])
+    tail = lines.reshape(n, -1)
     at = 0
     for i, length in zip(vectors, lengths):
         gathered[i] = tail[:, at : at + length].reshape(-1)
@@ -612,26 +693,27 @@
     input_grad, grads = backward_pass(gathered, saved, cotangent)
 
     low = jnp.bfloat16
-    blocks = []
-    for i in matrices:
-        rows, columns = params[i].shape
-        grad = grads[i].astype(low)
-        for c in range(columns // width):
-            blocks.append(grad[:, c * width : (c + 1) * width].reshape(n, rows, width))
-    lines = [grads[i].astype(low).reshape(n, -1) for i in vectors] + [jnp.zeros((n, spare), low)]
-    blocks.append(jnp.concatenate(lines, axis=1).reshape(n, total - row, width))
-    summed = reduce_all(jnp.concatenate(blocks, axis=1))
+    blocks = [grads[i].astype(low).reshape((n,) + a.shape) for i, a in zip(matrices, sent)]
+    parts = [grads[i].reshape(n, -1) for i in vectors] + [jnp.zeros((n, spare), jnp.float32)]
+    blocks.append(jnp.concatenate(parts, axis=1).reshape(n, tall, LANES))
+    sums, tail = reduce_all(blocks, n, width)
+
+    def joined(pieces):
+        return jnp.swapaxes(pieces, 0, 1).reshape(rows, -1).astype(jnp.float32)
 
     results = [None] * len(params)
-    for i in matrices:
-        rows = params[i].shape[0]
-        results[i] = jnp.concatenate([summed[r : r + rows] for r in place[i]], axis=1).astype(
-            jnp.float32
-        )
-    tail = summed[row:].reshape(-1)
+    whole = (
+        joined(sums[0, :3]),
+        sums[0, 3].astype(jnp.float32),
+        joined(sums[1]),
+        sums[2].reshape(4 * rows, width).astype(jnp.float32),
+    )
+    for i, array in zip(matrices, whole):
+        results[i] = array
+    tail = tail.reshape(-1)
     at = 0
     for i, length in zip(vectors, lengths):
-        results[i] = tail[at : at + length].astype(jnp.float32)
+        results[i] = tail[at : at + length]
         at += length
     return (output, input_grad, *results)
 

time: 257 us -> 230 us (0.89)
  local copies, waits for them, and re-layouts: 38.8 us -> 16 us
  Pallas kernels: 153 us -> 133 us
  matrix products: 52.8 us -> 65.2 us
  other arithmetic: 9.43 us -> 12.7 us
    pallas_call x2, Pallas kernels: 153 us -> 133 us  [the longest x1 73.9 us: reduce_all(): pl.pallas_call(functools.partial(reduce_kernel, n, width), out_shape=[jax...]
    unnamed x94 -> x86, local copies, waits for them, and re-layouts: 19.8 us -> 2.21 us
    slice x5 -> x2, local copies, waits for them, and re-layouts: 12.5 us -> 1.25 us  [per_device(): results[i] = tail[at:at + length]]
    dot_general x4, matrix products: 4.85 us -> 13.7 us  [outer_product(): jnp.dot(operand.reshape(-1, operand.shape[-1]).T, factor.reshape(-1, fact...]
    concatenate x1, local copies, waits for them, and re-layouts: 0.1 us -> 6.75 us  [per_device(): jnp.concatenate([params[i] for i in vectors] + [jnp.zeros(spare, params[0...]
where the time goes in v2:
time: 230 us; the launch traced here: 229 us
  Pallas kernels  133 us (58%)
  matrix products  65.2 us (28%)
  local copies, waits for them, and re-layouts  16 us (7%)
  other arithmetic  12.7 us (6%)
    pallas_call x1, Pallas kernels, reduce_all(): pl.pallas_call(functools.partial(reduce_kernel, n, width), out_shape=[jax...  73.9 us
    pallas_call x1, Pallas kernels, gather_all(): pl.pallas_call(functools.partial(gather_kernel, n, width), out_shape=[jax...  59.4 us
    dot_general x6, matrix products, batched(): return jnp.einsum(form, operand, factor, preferred_element_type=jnp.float32)  24.8 us
    dot_general x8, matrix products, matmul(): product = jnp.dot(flat, factor, preferred_element_type=jnp.float32)  24.1 us
    dot_general x4, matrix products, outer_product(): jnp.dot(operand.reshape(-1, operand.shape[-1]).T, factor.reshape(-1, fact...  13.7 us
    concatenate x1, local copies, waits for them, and re-layouts, per_device(): jnp.concatenate([params[i] for i in vectors] + [jnp.zeros(spare, params[0...  6.75 us

profile of v2, /device:TPU:0, one launch (start us, length us, event | category | flops | bytes accessed | tf_op | source)
XLA Modules:
  0.0 229.0 jit_solution(17038338382797987706)
XLA Ops:
  0.7 6.8 %concatenate.19 = bf16[2048]{0:T(1024)(128)(2,1)} concatenate(bf16[96]{0:T(256)(128)(2,1)} %param.19, bf16[96]{0:T(256)(128)(2,1)} %param.20, bf16[96]{0:T(256)(128)(2,1)} %param.22, bf16[96]{0:T(256)(128)(2,1)} %param.23, bf16[96]{0:T(256)(128)(2,1)} %param.25, bf16[96]{0:T(256)(128)(2,1)} %param.26, bf16[96]{0:T(256)(128)(2,1)} %param.27, bf16[384]{0:T(512)(128)(2,1)} %param.29, ...), dimensions={0} | concatenate | bytes 8192 | tf_op jit(solution)/shard_map/concatenate | solution.py:679
  7.4 59.4 %gather_all.1 = (bf16[8,96,2304]{2,1,0:T(8,128)(2,1)}, bf16[8,96,768]{2,1,0:T(8,128)(2,1)}, bf16[8,96,3072]{2,1,0:T(8,128)(2,1)}, bf16[8,4,96,768]{3,2,1,0:T(8,128)(2,1)}, bf16[8,16,128]{2,1,0:T(8,128)(2,1)}) custom-call(bf16[96,2304]{1,0:T(8,128)(2,1)} %qkv_in.1, bf16[96,768]{1,0:T(8,128)(2,1)} %out_in.1, bf16[96,3072]{1,0:T(8,128)(2,1)} %up_in.1, ...), custom_call_target="tpu_custom_call" | custom-call | tf_op jit(solution)/shard_map/gather_all/pallas_call | solution.py:412
  66.8 0.8 copy.64
  67.6 0.6 copy-done.12
  68.2 0.7 slice_convert_fusion.2
  68.9 0.1 reshape.489
  68.9 0.1 reshape.490
  69.0 1.1 convert_reduce_fusion
  70.1 1.2 fusion.49
  71.4 3.0 %convolution_bitcast_fusion = f32[1,197,2304]{2,1,0:T(8,128)S(1)} fusion(bf16[768,2304]{1,0:T(8,128)(2,1)} %bitcast.160, bf16[1,197,768]{2,1,0:T(8,128)(2,1)S(1)} %copy-done, f32[768]{0:T(1024)S(1)} %reshape.490, f32[768]{0:T(1024)S(1)} %reshape.489, f32[197]{0:T(256)S(1)} %add_rsqrt_fusion.1, f32[197]{0:T(256)S(1)} %broadcast_multiply_fusion.5), kind=kOutput, calls=%fused_computation.5 | convolution fusion | flops 698079744 | bytes 5664808 | tf_op jit(solution)/shard_map/dot_general | solution.py:20
  74.4 0.1 reshape.491
  74.5 0.1 reshape.492
  74.5 0.1 fusion.50
  74.6 0.2 copy.44
  74.8 0.2 copy.45
  75.0 2.0 fusion.114
  77.0 0.2 copy.43
  77.2 3.7 %convolution_convert_fusion.4 = bf16[12,64,197]{2,1,0:T(8,128)(2,1)S(1)} fusion(bf16[197,12,64]{0,2,1:T(8,128)(2,1)S(1)} %bitcast.168, f32[12,197,197]{1,2,0:T(8,128)} %fusion.114), kind=kOutput, calls=%fused_computation.31 | convolution fusion | flops 61627312 | bytes 2468016 | tf_op jit(solution)/shard_map/bhqk,bkhd->bqhd/dot_general | solution.py:33
  80.9 0.1 reshape.493
  80.9 0.5 fusion.108
  81.5 0.2 multiply_reduce_fusion.1
  81.7 0.1 reshape.494
  81.8 0.1 reshape.495
  81.9 0.8 slice_convert_fusion.1
  82.7 3.6 %multiply_convert_fusion.1 = (bf16[197,3072]{1,0:T(8,128)(2,1)S(1)}, f32[197,3072]{1,0:T(8,128)S(1)}) fusion(f32[3072]{0:T(1024)S(1)} %reshape.496, bf16[768,3072]{1,0:T(8,128)(2,1)} %bitcast.155, f32[1,197,768]{2,1,0:T(8,128)S(1)} %get-tuple-element.65, f32[768]{0:T(1024)S(1)} %reshape.495, f32[768]{0:T(1024)S(1)} %reshape.494, f32[197]{0:T(256)S(1)} %add_rsqrt_fusion, ...), kind=kOutput, calls=%fused_computation.18 | convolution fusion | flops 933950208 | bytes 8974888 | tf_op jit(solution)/shard_map/dot_general | solution.py:20
  87.0 4.8 %fusion.113 = (f32[3072]{0:T(1024)}, bf16[197,3072]{1,0:T(8,128)(2,1)S(1)}) fusion(f32[197,3072]{1,0:T(8,128)S(1)} %get-tuple-element.67, bf16[3072,768]{1,0:T(8,128)(2,1)} %bitcast.185, bf16[1,197,768]{2,1,0:T(8,128)(2,1)S(1)} %copy-done.8, f32[]{:T(128)} %bitcast.17), kind=kOutput, calls=%fused_computation.136 | convolution fusion | flops 936670464 | bytes 8664580 | tf_op jit(solution)/shard_map/dot_general | solution.py:20
  91.8 2.3 %fusion.52 = (f32[768]{0:T(1024)}, f32[197]{0:T(256)S(1)}, f32[197,768]{1,0:T(8,128)S(1)}) fusion(f32[1,197,768]{2,1,0:T(8,128)S(1)} %get-tuple-element.65, f32[197]{0:T(256)S(1)} %add_rsqrt_fusion, f32[197]{0:T(256)S(1)} %broadcast_multiply_fusion.4, f32[768]{0:T(1024)S(1)} %reshape.494, bf16[768,3072]{1,0:T(8,128)(2,1)S(1)} %bitcast.158, ...), kind=kOutput, calls=%fused_computation.68 | convolution fusion | flops 930620736 | bytes 7147836 | tf_op jit(solution)/shard_map/dot_general | solution.py:20
  94.1 0.7 fusion.100
  94.8 1.6 fusion.102
  96.4 1.3 convolution_convert_fusion.5
  97.7 1.9 copy.47
  99.6 3.0 %fusion.115 = f32[12,197,197]{1,2,0:T(8,128)} fusion(bf16[197,12,64]{0,2,1:T(8,128)(2,1)} %bitcast.170, bf16[197,12,64]{0,2,1:T(8,128)(2,1)} %bitcast.169), kind=kOutput, calls=%fused_computation.138 | convolution fusion | flops 59610624 | bytes 2468016 | tf_op jit(solution)/shard_map/bqhd,bkhd->bhqk/dot_general | solution.py:33
  102.6 2.6 %fusion.6 = f32[12,197,197]{1,2,0:T(8,128)} fusion(bf16[197,12,64]{0,2,1:T(8,128)(2,1)S(1)} %bitcast.163, bf16[197,12,64]{0,2,1:T(8,128)(2,1)S(1)} %bitcast.166), kind=kOutput, calls=%fused_computation.14 | convolution fusion | flops 120620928 | bytes 2468016 | tf_op jit(solution)/shard_map/reduce_sum | solution.py:96
  105.2 6.0 %fusion.106 = (f32[12,64]{1,0:T(8,128)}, bf16[1,197,12,64]{1,3,2,0:T(8,128)(2,1)}) fusion(bf16[197,12,64]{0,2,1:T(8,128)(2,1)S(1)} %bitcast.167, f32[12,197,197]{1,2,0:T(8,128)} %fusion.6, f32[12,197,197]{1,2,0:T(8,128)} %fusion.115), kind=kOutput, calls=%fused_computation.133 | convolution fusion | flops 62243548 | bytes 4333920 | tf_op jit(solution)/shard_map/bhqk,bkhd->bqhd/dot_general | solution.py:33
  111.2 5.4 %fusion.23 = bf16[12,64,197]{2,1,0:T(8,128)(2,1)} fusion(bf16[197,12,64]{0,2,1:T(8,128)(2,1)S(1)} %bitcast.164, f32[12,197,197]{1,2,0:T(8,128)} %fusion.6, f32[12,197,197]{1,2,0:T(8,128)} %fusion.115), kind=kOutput, calls=%fused_computation.30 | convolution fusion | flops 62093020 | bytes 4330848 | tf_op jit(solution)/shard_map/bhqk,bqhd->bkhd/dot_general | solution.py:33
  116.6 4.7 %fusion.105 = (f32[12,64]{1,0:T(8,128)}, bf16[1,197,12,64]{1,3,2,0:T(8,128)(2,1)}) fusion(bf16[197,12,64]{0,2,1:T(8,128)(2,1)S(1)} %bitcast.171, f32[12,197,197]{1,2,0:T(8,128)} %fusion.114), kind=kOutput, calls=%fused_computation.132 | convolution fusion | flops 61777840 | bytes 2471088 | tf_op jit(solution)/shard_map/bhqk,bqhd->bkhd/dot_general | solution.py:33
  121.4 4.4 %fusion.48 = (f32[768]{0:T(1024)S(1)}, f32[197]{0:T(256)}, f32[197,768]{1,0:T(8,128)S(1)}) fusion(bf16[1,197,768]{2,1,0:T(8,128)(2,1)S(1)} %copy-done, f32[197]{0:T(256)} %copy-done.30, f32[197]{0:T(256)} %copy-done.19, f32[768]{0:T(1024)} %copy-done.13, bf16[768,2304]{1,0:T(8,128)(2,1)} %bitcast.161, bf16[197,768]{0,1:T(8,128)(2,1)} %bitcast.191, ...), kind=kOutput, calls=%fused_computation.60 | convolution fusion | flops 701104704 | bytes 5363004 | tf_op jit(solution)/shard_map/dot_general | solution.py:20
  125.8 0.2 fusion.101
  126.0 0.1 reshape.478
  126.1 0.1 reshape.477
  126.1 0.1 reshape.479
  126.2 0.1 reshape.480
  126.3 0.1 reshape.481
  126.4 0.1 reshape.486
  126.4 0.1 reshape.484
  126.5 0.1 reshape.483
  126.6 0.1 concatenate.24
  126.7 0.6 copy.63
  127.4 5.1 %convolution_convert_fusion.1 = bf16[768,3072]{1,0:T(8,128)(2,1)} fusion(bf16[197,3072]{1,0:T(8,128)(2,1)} %copy-done.7, f32[1,197,768]{2,1,0:T(8,128)S(1)} %get-tuple-element.65, f32[768]{0:T(1024)S(1)} %copy-done.11, f32[768]{0:T(1024)S(1)} %reshape.494, f32[197]{0:T(256)S(1)} %copy-done.18, f32[197]{0:T(256)S(1)} %copy-done.16), kind=kOutput, calls=%fused_computation.3 | convolution fusion | flops 932678400 | bytes 6541864 | tf_op jit(solution)/shard_map/dot_general | solution.py:25
  132.6 1.5 convolution_convert_fusion.3
  134.1 3.3 %convolution_convert_fusion.2 = bf16[768,2304]{1,0:T(8,128)(2,1)} fusion(bf16[197,768]{0,1:T(8,128)(2,1)S(1)} %bitcast.192, bf16[197,768]{0,1:T(8,128)(2,1)S(1)} %bitcast.190, bf16[197,768]{0,1:T(8,128)(2,1)S(1)} %bitcast.188, bf16[1,197,768]{2,1,0:T(8,128)(2,1)S(1)} %copy-done, f32[768]{0:T(1024)S(1)} %copy-done.22, f32[768]{0:T(1024)S(1)} %copy-done.14, ...), kind=kOutput, calls=%fused_computation.4 | convolution fusion | flops 702572544 | bytes 4757032 | tf_op jit(solution)/shard_map/dot_general | solution.py:25
  137.4 3.7 %convolution_convert_fusion = bf16[3072,768]{1,0:T(8,128)(2,1)} fusion(bf16[197,3072]{1,0:T(8,128)(2,1)S(1)} %get-tuple-element.66, bf16[1,197,768]{2,1,0:T(8,128)(2,1)S(1)} %copy-done.9, f32[]{:T(128)} %bitcast.17), kind=kOutput, calls=%fused_computation.2 | convolution fusion | flops 932375808 | bytes 6231556 | tf_op jit(solution)/shard_map/dot_general | solution.py:25
  141.2 73.9 %reduce_all.1 = (bf16[3,4,96,768]{3,2,1,0:T(8,128)(2,1)}, f32[16,128]{1,0:T(8,128)}) custom-call(bf16[8,96,2304]{2,1,0:T(8,128)(2,1)} %bitcast.159, bf16[8,96,768]{2,1,0:T(8,128)(2,1)} %bitcast.152, bf16[8,96,3072]{2,1,0:T(8,128)(2,1)} %bitcast.151, bf16[8,4,96,768]{3,2,1,0:T(8,128)(2,1)} %bitcast.150, f32[8,16,128]{2,1,0:T(8,128)} %bitcast.177), custom_call_target="tpu_custom_call" | custom-call | tf_op jit(solution)/shard_map/reduce_all/pallas_call | solution.py:625
  215.1 1.4 fusion.104
  216.5 1.1 copy.58
  217.6 1.1 bitcast_convert_fusion
  218.8 1.1 convert_bitcast_fusion.1
  219.8 1.0 copy.57
  220.8 1.6 bitcast_convert_fusion.1
  222.5 0.6 fusion.107
  223.1 0.6 slice.120
  223.7 1.0 fusion.47
  224.7 0.1 reshape.497
  224.8 4.2 %fusion.34 = bf16[1,197,768]{2,1,0:T(8,128)(2,1)} fusion(f32[1,197,768]{2,1,0:T(8,128)S(1)} %get-tuple-element.65, bf16[197,3072]{1,0:T(8,128)(2,1)S(1)} %get-tuple-element.66, bf16[3072,768]{1,0:T(8,128)(2,1)} %bitcast.186, f32[]{:T(128)} %bitcast.17, f32[768]{0:T(1024)S(1)} %reshape.497), kind=kOutput, calls=%fused_computation.40 | convolution fusion | flops 930167808 | bytes 6839812 | tf_op jit(solution)/shard_map/dot_general | solution.py:20
  (96 shorter events, 0.3 us)
Async XLA Ops:
  0.6 70.7 %copy-start = (bf16[1,197,768]{2,1,0:T(8,128)(2,1)S(1)}, bf16[1,197,768]{2,1,0:T(8,128)(2,1)}, u32[]{:S(2)}) copy-start(bf16[1,197,768]{2,1,0:T(8,128)(2,1)} %param.16) | copy-start | bytes 907780
  67.6 0.6 copy-start.12
  68.9 5.4 %copy-start.13 = (f32[768]{0:T(1024)}, f32[768]{0:T(1024)S(1)}, u32[]{:S(2)}) copy-start(f32[768]{0:T(1024)S(1)} %reshape.489) | copy-start | bytes 9220
  69.0 5.3 %copy-start.21 = (f32[768]{0:T(1024)}, f32[768]{0:T(1024)S(1)}, u32[]{:S(2)}) copy-start(f32[768]{0:T(1024)S(1)} %reshape.490) | copy-start | bytes 9220
  70.1 4.3 %copy-start.19 = (f32[197]{0:T(256)}, f32[197]{0:T(256)S(1)}, u32[]{:S(2)}) copy-start(f32[197]{0:T(256)S(1)} %broadcast_multiply_fusion.5) | copy-start | bytes 2368
  71.3 3.0 %copy-start.30 = (f32[197]{0:T(256)}, f32[197]{0:T(256)S(1)}, u32[]{:S(2)}) copy-start(f32[197]{0:T(256)S(1)} %add_rsqrt_fusion.1) | copy-start | bytes 2368
  77.0 4.0 %copy-start.1 = (bf16[8,96,768]{2,1,0:T(8,128)(2,1)S(1)}, bf16[8,96,768]{2,1,0:T(8,128)(2,1)}, u32[]{:S(2)}) copy-start(bf16[8,96,768]{2,1,0:T(8,128)(2,1)} %get-tuple-element.24) | copy-start | bytes 3538948
  77.2 3.8 %copy-start.3 = (bf16[1,197,768]{1,2,0:T(8,128)(2,1)}, bf16[1,197,768]{1,2,0:T(8,128)(2,1)S(1)}, u32[]{:S(2)}) copy-start(bf16[1,197,768]{1,2,0:T(8,128)(2,1)S(1)} %copy.43) | copy-start | bytes 907780
  80.8 1.9 copy-start.5
  80.8 0.9 copy-start.28
  80.8 1.0 copy-start.27
  81.5 10.3 %copy-start.15 = (f32[197]{0:T(256)}, f32[197]{0:T(256)S(1)}, u32[]{:S(2)}) copy-start(f32[197]{0:T(256)S(1)} %broadcast_multiply_fusion.4) | copy-start | bytes 2368
  81.7 10.1 %copy-start.17 = (f32[197]{0:T(256)}, f32[197]{0:T(256)S(1)}, u32[]{:S(2)}) copy-start(f32[197]{0:T(256)S(1)} %add_rsqrt_fusion) | copy-start | bytes 2368
  81.9 4.4 %copy-start.10 = (f32[768]{0:T(1024)}, f32[768]{0:T(1024)S(1)}, u32[]{:S(2)}) copy-start(f32[768]{0:T(1024)S(1)} %reshape.495) | copy-start | bytes 9220
  82.7 4.3 %copy-start.8 = (bf16[1,197,768]{2,1,0:T(8,128)(2,1)S(1)}, bf16[1,197,768]{2,1,0:T(8,128)(2,1)}, u32[]{:S(2)}) copy-start(bf16[1,197,768]{2,1,0:T(8,128)(2,1)} %param.17) | copy-start | bytes 907780
  82.7 9.1 %slice-start = ((s8[4718592]{0:T(1024)(128)(4,1)}), s8[4194304]{0:T(1024)(128)(4,1)S(1)}, s32[]{:S(2)}) async-start(s8[4718592]{0:T(1024)(128)(4,1)} %bitcast.156), calls=%async_computation | async-start | bytes 8388608
  87.0 4.8 %slice-start.1 = ((s8[4718592]{0:T(1024)(128)(4,1)}), s8[524288]{0:T(1024)(128)(4,1)S(1)}, s32[]{:S(2)}) async-start(s8[4718592]{0:T(1024)(128)(4,1)} %bitcast.156), calls=%async_computation.1 | async-start | bytes 1048576
  91.8 2.3 %copy-start.7 = (bf16[197,3072]{1,0:T(8,128)(2,1)}, bf16[197,3072]{1,0:T(8,128)(2,1)S(1)}, u32[]{:S(2)}) copy-start(bf16[197,3072]{1,0:T(8,128)(2,1)S(1)} %get-tuple-element.73) | copy-start | bytes 3631108
  94.1 2.3 copy-start.2
  111.2 5.4 %copy-start.4 = (bf16[197,768]{0,1:T(8,128)(2,1)S(1)}, bf16[197,768]{0,1:T(8,128)(2,1)}, u32[]{:S(2)}) copy-start(bf16[197,768]{0,1:T(8,128)(2,1)} %copy.47) | copy-start | bytes 907780
  121.4 4.5 %copy-start.14 = (f32[768]{0:T(1024)S(1)}, f32[768]{0:T(1024)}, u32[]{:S(2)}) copy-start(f32[768]{0:T(1024)} %copy-done.13) | copy-start | bytes 9220
  121.4 4.8 %copy-start.32 = (f32[12,64]{1,0:T(8,128)S(1)}, f32[12,64]{1,0:T(8,128)}, u32[]{:S(2)}) copy-start(f32[12,64]{1,0:T(8,128)} %get-tuple-element.45) | copy-start | bytes 9220
  121.4 4.8 %copy-start.33 = (f32[12,64]{1,0:T(8,128)S(1)}, f32[12,64]{1,0:T(8,128)}, u32[]{:S(2)}) copy-start(f32[12,64]{1,0:T(8,128)} %get-tuple-element.43) | copy-start | bytes 9220
  121.4 4.9 %copy-start.25 = (f32[768]{0:T(1024)S(1)}, f32[768]{0:T(1024)}, u32[]{:S(2)}) copy-start(f32[768]{0:T(1024)} %get-tuple-element.37) | copy-start | bytes 9220
  121.4 5.0 %copy-start.24 = (f32[768]{0:T(1024)S(1)}, f32[768]{0:T(1024)}, u32[]{:S(2)}) copy-start(f32[768]{0:T(1024)} %get-tuple-element.47) | copy-start | bytes 9220
  121.4 5.1 %copy-start.23 = (f32[768]{0:T(1024)S(1)}, f32[768]{0:T(1024)}, u32[]{:S(2)}) copy-start(f32[768]{0:T(1024)} %get-tuple-element.33) | copy-start | bytes 9220
  121.4 5.1 %copy-start.35 = (f32[768]{0:T(1024)S(1)}, f32[768]{0:T(1024)}, u32[]{:S(2)}) copy-start(f32[768]{0:T(1024)} %get-tuple-element.29) | copy-start | bytes 9220
  121.4 5.2 %copy-start.29 = (f32[3072]{0:T(1024)S(1)}, f32[3072]{0:T(1024)}, u32[]{:S(2)}) copy-start(f32[3072]{0:T(1024)} %get-tuple-element.72) | copy-start | bytes 36868
  121.4 5.9 %copy-start.11 = (f32[768]{0:T(1024)S(1)}, f32[768]{0:T(1024)}, u32[]{:S(2)}) copy-start(f32[768]{0:T(1024)} %copy-done.10) | copy-start | bytes 9220
  121.4 5.9 %copy-start.16 = (f32[197]{0:T(256)S(1)}, f32[197]{0:T(256)}, u32[]{:S(2)}) copy-start(f32[197]{0:T(256)} %copy-done.15) | copy-start | bytes 2368
  121.4 5.9 %copy-start.18 = (f32[197]{0:T(256)S(1)}, f32[197]{0:T(256)}, u32[]{:S(2)}) copy-start(f32[197]{0:T(256)} %copy-done.17) | copy-start | bytes 2368
  127.4 5.2 %copy-start.6 = (bf16[12,64,197]{2,1,0:T(8,128)(2,1)S(1)}, bf16[12,64,197]{2,1,0:T(8,128)(2,1)}, u32[]{:S(2)}) copy-start(bf16[12,64,197]{2,1,0:T(8,128)(2,1)} %copy-done.5) | copy-start | bytes 907780
  127.4 6.7 %copy-start.20 = (f32[197]{0:T(256)S(1)}, f32[197]{0:T(256)}, u32[]{:S(2)}) copy-start(f32[197]{0:T(256)} %copy-done.19) | copy-start | bytes 2368
  127.4 6.7 %copy-start.22 = (f32[768]{0:T(1024)S(1)}, f32[768]{0:T(1024)}, u32[]{:S(2)}) copy-start(f32[768]{0:T(1024)} %copy-done.21) | copy-start | bytes 9220
  127.4 6.7 %copy-start.31 = (f32[197]{0:T(256)S(1)}, f32[197]{0:T(256)}, u32[]{:S(2)}) copy-start(f32[197]{0:T(256)} %copy-done.30) | copy-start | bytes 2368
  127.4 6.7 %copy-start.37 = (bf16[1,197,12,64]{1,3,2,0:T(8,128)(2,1)S(1)}, bf16[1,197,12,64]{1,3,2,0:T(8,128)(2,1)}, u32[]{:S(2)}) copy-start(bf16[1,197,12,64]{1,3,2,0:T(8,128)(2,1)} %get-tuple-element.46) | copy-start | bytes 907780
  127.4 6.7 %copy-start.38 = (bf16[12,64,197]{2,1,0:T(8,128)(2,1)S(1)}, bf16[12,64,197]{2,1,0:T(8,128)(2,1)}, u32[]{:S(2)}) copy-start(bf16[12,64,197]{2,1,0:T(8,128)(2,1)} %fusion.23) | copy-start | bytes 907780
  127.4 6.7 %copy-start.39 = (bf16[1,197,12,64]{1,3,2,0:T(8,128)(2,1)S(1)}, bf16[1,197,12,64]{1,3,2,0:T(8,128)(2,1)}, u32[]{:S(2)}) copy-start(bf16[1,197,12,64]{1,3,2,0:T(8,128)(2,1)} %get-tuple-element.44) | copy-start | bytes 907780
  134.1 3.3 %copy-start.9 = (bf16[1,197,768]{2,1,0:T(8,128)(2,1)S(1)}, bf16[1,197,768]{2,1,0:T(8,128)(2,1)}, u32[]{:S(2)}) copy-start(bf16[1,197,768]{2,1,0:T(8,128)(2,1)} %param.17) | copy-start | bytes 907780
  217.6 4.8 %copy-start.34 = (f32[16,128]{1,0:T(8,128)S(1)}, f32[16,128]{1,0:T(8,128)}, u32[]{:S(2)}) copy-start(f32[16,128]{1,0:T(8,128)} %get-tuple-element.27) | copy-start | bytes 24580
  217.6 6.1 %copy-start.36 = (f32[197]{0:T(256)S(1)}, f32[197]{0:T(256)}, u32[]{:S(2)}) copy-start(f32[197]{0:T(256)} %get-tuple-element.32) | copy-start | bytes 2368
  218.8 6.0 %copy-start.26 = (f32[8,96]{1,0:T(8,128)S(1)}, f32[8,96]{1,0:T(8,128)}, u32[]{:S(2)}) copy-start(f32[8,96]{1,0:T(8,128)} %get-tuple-element.48) | copy-start | bytes 9220
